TPU v7x, 32 devices: a whole 2x2x4 slice. The times are simulated.
32 devices in a mesh: fsdp: 32 (over z, y, x, core).
Axes of the slice: x: 2, y: 2, z: 4, core: 2. Of those that a mesh axis runs over, the one named last changes fastest.
Arguments:
- tokens: bfloat16 [32768, 640], P('fsdp'), may hold values from -6 to 6
- cotangent: bfloat16 [32768, 640], P('fsdp'), may hold values from -6 to 6
- seq_lens: int32 [128], P('fsdp'), may hold values from 0 to 1024, as said below
- seq_starts: int32 [128], P('fsdp'), may hold values from 0 to 1024, as said below
- input_gain: bfloat16 [640], P('fsdp'), may hold values from 0.099609375 to 1.8984375
- w_query: bfloat16 [640, 1024], P('fsdp'), may hold values from -0.25 to 0.25
- w_key: bfloat16 [640, 256], P('fsdp'), may hold values from -0.25 to 0.25
- w_value: bfloat16 [640, 256], P('fsdp'), may hold values from -0.25 to 0.25
- query_gain: bfloat16 [256], P('fsdp'), may hold values from 0.099609375 to 1.8984375
- key_gain: bfloat16 [256], P('fsdp'), may hold values from 0.099609375 to 1.8984375
- w_output: bfloat16 [1024, 640], P('fsdp'), may hold values from -0.1875 to 0.1875
- attn_post_gain: bfloat16 [640], P('fsdp'), may hold values from 0.099609375 to 1.8984375
- ffn_pre_gain: bfloat16 [640], P('fsdp'), may hold values from 0.099609375 to 1.8984375
- w_gate: bfloat16 [640, 2048], P('fsdp'), may hold values from -0.25 to 0.25
- w_up: bfloat16 [640, 2048], P('fsdp'), may hold values from -0.25 to 0.25
- w_down: bfloat16 [2048, 640], P('fsdp'), may hold values from -0.125 to 0.125
- ffn_post_gain: bfloat16 [640], P('fsdp'), may hold values from 0.099609375 to 1.8984375
Outputs:
- result: bfloat16 [32768, 640], P('fsdp')
- grad_tokens: float32 [32768, 640], P('fsdp')
- grad_input_gain: float32 [640], P('fsdp')
- grad_w_query: float32 [640, 1024], P('fsdp')
- grad_w_key: float32 [640, 256], P('fsdp')
- grad_w_value: float32 [640, 256], P('fsdp')
- grad_query_gain: float32 [256], P('fsdp')
- grad_key_gain: float32 [256], P('fsdp')
- grad_w_output: float32 [1024, 640], P('fsdp')
- grad_attn_post_gain: float32 [640], P('fsdp')
- grad_ffn_pre_gain: float32 [640], P('fsdp')
- grad_w_gate: float32 [640, 2048], P('fsdp')
- grad_w_up: float32 [640, 2048], P('fsdp')
- grad_w_down: float32 [2048, 640], P('fsdp')
- grad_ffn_post_gain: float32 [640], P('fsdp')
Inputs may be any that keep to these rules, and one draw needn't show every extreme that they name: `seq_lens`: on each device its 4 sequence slots lie end to end from token slot 0 in the order given, so seq_starts is the sum of the lengths before it on that device; a length may be 0; every device has 256 or more slots inside sequences; some device holds one sequence of exactly 1024 tokens, filling it. `seq_starts`: the start of each sequence slot, as described for seq_lens.
All inputs are finite; a program needn't handle non-finite values.
Results may differ from a plain program's by a relative error of at most 0.017.
Values may be sent and summed in bfloat16 or wider, within the bound.
No kernel may reach another device: no remote copies, remote signals or barrier semaphores. Data moves between devices by JAX's collectives and lax.ppermute only.
A program may use at most 192 MiB of HBM per device.

v0:
```python
import jax
import jax.numpy as jnp
from jax import lax
from jax.sharding import PartitionSpec as P

epsilon = 1e-06
rope_base = 1000000.0


def product(left_side, right_side):
    return jnp.dot(left_side, right_side, preferred_element_type=jnp.float32)


def times_transposed(left_side, right_side):
    return lax.dot_general(
        left_side, right_side, (((1,), (1,)), ((), ())), preferred_element_type=jnp.float32
    )


def outer_sum(left_side, right_side):
    return lax.dot_general(
        left_side, right_side, (((0,), (0,)), ((), ())), preferred_element_type=jnp.float32
    )


def rms_scale(vector_rows, gain_row):
    return (
        vector_rows
        * lax.rsqrt(jnp.mean(vector_rows * vector_rows, axis=-1, keepdims=True) + epsilon)
        * gain_row
    )


def rotate(vector_rows, positions):
    half_width = vector_rows.shape[-1] // 2
    frequency = rope_base ** (
        -2.0 * jnp.arange(half_width, dtype=jnp.float32) / vector_rows.shape[-1]
    )
    angles = positions[:, None] * frequency[None, :]
    if vector_rows.ndim == 3:
        angles = angles[:, None, :]
    cosine = jnp.cos(angles)
    sine_part = jnp.sin(angles)
    first_half = vector_rows[..., :half_width]
    second_half = vector_rows[..., half_width:]
    return jnp.concatenate(
        [
            first_half * cosine - second_half * sine_part,
            second_half * cosine + first_half * sine_part,
        ],
        axis=-1,
    )


def prep_query(raw_rows, gain_row, positions):
    shaped = raw_rows.reshape(raw_rows.shape[0], -1, gain_row.shape[0])
    return rotate(rms_scale(shaped, gain_row), positions) * 0.0625


def prep_key(raw_rows, gain_row, positions):
    return rotate(rms_scale(raw_rows, gain_row), positions)


def glu_mix(gating, upward):
    return jax.nn.gelu(gating, approximate=True) * upward


def layout(lengths, starts, slot_count):
    slot_index = jnp.arange(slot_count, dtype=jnp.int32)
    inside = (slot_index[None, :] >= starts[:, None]) & (
        slot_index[None, :] < starts[:, None] + lengths[:, None]
    )
    member = inside.astype(jnp.float32)
    live_mask = jnp.sum(member, axis=0)
    offset = jnp.sum(member * starts[:, None].astype(jnp.float32), axis=0)
    positions = slot_index.astype(jnp.float32) - offset
    same_seq = jnp.dot(member.T, member, preferred_element_type=jnp.float32) > 0.5
    allowed = same_seq & (slot_index[None, :] <= slot_index[:, None]) | (
        slot_index[None, :] == slot_index[:, None]
    )
    return (live_mask, positions, allowed)


def attend(queries, key_rows, value_rows, allowed):
    scores = jnp.einsum("thd,ud->htu", queries, key_rows, preferred_element_type=jnp.float32)
    masked = jnp.where(allowed[None], scores, -1e30)
    row_peak = jnp.max(masked, axis=-1, keepdims=True)
    exponent = jnp.exp(masked - row_peak)
    row_total = jnp.sum(exponent, axis=-1, keepdims=True)
    probability = (exponent / row_total).astype(jnp.bfloat16)
    mixture = jnp.einsum("htu,ud->thd", probability, value_rows, preferred_element_type=jnp.float32)
    return (mixture, row_peak + jnp.log(row_total))


def attend_back(queries, key_rows, value_rows, allowed, log_total, grad_mixture):
    scores = jnp.einsum("thd,ud->htu", queries, key_rows, preferred_element_type=jnp.float32)
    masked = jnp.where(allowed[None], scores, -1e30)
    probability = jnp.exp(masked - log_total)
    weights_low = probability.astype(jnp.bfloat16)
    grad_probs = jnp.einsum(
        "thd,ud->htu", grad_mixture, value_rows, preferred_element_type=jnp.float32
    )
    grad_values = jnp.einsum(
        "htu,thd->ud", weights_low, grad_mixture, preferred_element_type=jnp.float32
    )
    row_inner = jnp.sum(probability * grad_probs, axis=-1, keepdims=True)
    grad_scores = (probability * (grad_probs - row_inner)).astype(jnp.bfloat16)
    grad_queries = jnp.einsum(
        "htu,ud->thd", grad_scores, key_rows, preferred_element_type=jnp.float32
    )
    grad_keys = jnp.einsum("htu,thd->ud", grad_scores, queries, preferred_element_type=jnp.float32)
    return (grad_queries, grad_keys, grad_values)


def on_device(
    tokens,
    cotangent,
    seq_lens,
    seq_starts,
    input_gain,
    w_query,
    w_key,
    w_value,
    query_gain,
    key_gain,
    w_output,
    attn_post_gain,
    ffn_pre_gain,
    w_gate,
    w_up,
    w_down,
    ffn_post_gain,
):
    slot_count = tokens.shape[0]
    live_mask, positions, allowed = layout(seq_lens, seq_starts, slot_count)
    attn_whole = (
        lax.all_gather(input_gain, "fsdp", axis=0, tiled=True),
        lax.all_gather(w_query, "fsdp", axis=0, tiled=True),
        lax.all_gather(w_key, "fsdp", axis=0, tiled=True),
        lax.all_gather(w_value, "fsdp", axis=0, tiled=True),
        lax.all_gather(query_gain, "fsdp", axis=0, tiled=True),
        lax.all_gather(key_gain, "fsdp", axis=0, tiled=True),
        lax.all_gather(w_output, "fsdp", axis=0, tiled=True),
        lax.all_gather(attn_post_gain, "fsdp", axis=0, tiled=True),
    )
    gain_in = attn_whole[0].astype(jnp.float32)
    query_w = attn_whole[1]
    key_w = attn_whole[2]
    value_w = attn_whole[3]
    gain_q = attn_whole[4].astype(jnp.float32)
    gain_k = attn_whole[5].astype(jnp.float32)
    output_w = attn_whole[6]
    gain_post = attn_whole[7].astype(jnp.float32)
    head_count = query_w.shape[1] // key_w.shape[1]

    def query_piece(raw_rows, gain_row):
        return prep_query(raw_rows, gain_row, positions)

    def key_piece(raw_rows, gain_row):
        return prep_key(raw_rows, gain_row, positions)

    inputs = tokens.astype(jnp.float32)
    normed = rms_scale(inputs, gain_in).astype(jnp.bfloat16)
    query_raw = product(normed, query_w)
    key_raw = product(normed, key_w)
    value_low = product(normed, value_w).astype(jnp.bfloat16)
    query_low = query_piece(query_raw, gain_q).astype(jnp.bfloat16)
    key_low = key_piece(key_raw, gain_k).astype(jnp.bfloat16)
    mixture, log_total = attend(query_low, key_low, value_low, allowed)
    mixed_low = mixture.reshape(slot_count, -1).astype(jnp.bfloat16)
    attn_out = product(mixed_low, output_w)
    middle = inputs + rms_scale(attn_out, gain_post)
    ffn_whole = (
        lax.all_gather(ffn_pre_gain, "fsdp", axis=0, tiled=True),
        lax.all_gather(w_gate, "fsdp", axis=0, tiled=True),
        lax.all_gather(w_up, "fsdp", axis=0, tiled=True),
        lax.all_gather(w_down, "fsdp", axis=0, tiled=True),
        lax.all_gather(ffn_post_gain, "fsdp", axis=0, tiled=True),
    )
    gain_pre = ffn_whole[0].astype(jnp.float32)
    gain_ffn = ffn_whole[4].astype(jnp.float32)
    normed_ffn = rms_scale(middle, gain_pre).astype(jnp.bfloat16)
    gating = product(normed_ffn, ffn_whole[1])
    upward = product(normed_ffn, ffn_whole[2])
    active = glu_mix(gating, upward).astype(jnp.bfloat16)
    down_out = product(active, ffn_whole[3])
    output_rows = middle + rms_scale(down_out, gain_ffn)
    result = (live_mask[:, None] * output_rows).astype(jnp.bfloat16)
    grad_output = cotangent.astype(jnp.float32) * live_mask[:, None]
    ffn_back = (
        lax.all_gather(ffn_pre_gain, "fsdp", axis=0, tiled=True),
        lax.all_gather(w_gate, "fsdp", axis=0, tiled=True),
        lax.all_gather(w_up, "fsdp", axis=0, tiled=True),
        lax.all_gather(w_down, "fsdp", axis=0, tiled=True),
        lax.all_gather(ffn_post_gain, "fsdp", axis=0, tiled=True),
    )
    _, post_ffn_back = jax.vjp(rms_scale, down_out, ffn_back[4].astype(jnp.float32))
    grad_down_out, grad_gain_ffn = post_ffn_back(grad_output)
    grad_down_low = grad_down_out.astype(jnp.bfloat16)
    grad_active = times_transposed(grad_down_low, ffn_back[3])
    part_down = outer_sum(active, grad_down_low)
    _, glu_back = jax.vjp(glu_mix, gating, upward)
    grad_gating, grad_upward = glu_back(grad_active)
    grad_gate_low = grad_gating.astype(jnp.bfloat16)
    grad_up_low = grad_upward.astype(jnp.bfloat16)
    part_gate = outer_sum(normed_ffn, grad_gate_low)
    part_up = outer_sum(normed_ffn, grad_up_low)
    grad_normed_ffn = times_transposed(grad_gate_low, ffn_back[1]) + times_transposed(
        grad_up_low, ffn_back[2]
    )
    _, pre_ffn_back = jax.vjp(rms_scale, middle, ffn_back[0].astype(jnp.float32))
    grad_middle_part, grad_gain_pre = pre_ffn_back(grad_normed_ffn)
    grad_middle = grad_output + grad_middle_part
    ffn_owned = None
    attn_back = (
        lax.all_gather(input_gain, "fsdp", axis=0, tiled=True),
        lax.all_gather(w_query, "fsdp", axis=0, tiled=True),
        lax.all_gather(w_key, "fsdp", axis=0, tiled=True),
        lax.all_gather(w_value, "fsdp", axis=0, tiled=True),
        lax.all_gather(query_gain, "fsdp", axis=0, tiled=True),
        lax.all_gather(key_gain, "fsdp", axis=0, tiled=True),
        lax.all_gather(w_output, "fsdp", axis=0, tiled=True),
        lax.all_gather(attn_post_gain, "fsdp", axis=0, tiled=True),
    )
    _, post_attn_back = jax.vjp(rms_scale, attn_out, attn_back[7].astype(jnp.float32))
    grad_attn_out, grad_gain_post = post_attn_back(grad_middle)
    grad_attn_low = grad_attn_out.astype(jnp.bfloat16)
    part_output = outer_sum(mixed_low, grad_attn_low)
    grad_mixture = (
        times_transposed(grad_attn_low, attn_back[6])
        .astype(jnp.bfloat16)
        .reshape(slot_count, head_count, -1)
    )
    grad_queries, grad_keys, grad_values = attend_back(
        query_low, key_low, value_low, allowed, log_total, grad_mixture
    )
    grad_value_low = grad_values.astype(jnp.bfloat16)
    _, query_back = jax.vjp(query_piece, query_raw, attn_back[4].astype(jnp.float32))
    grad_query_raw, grad_gain_q = query_back(grad_queries)
    _, key_back = jax.vjp(key_piece, key_raw, attn_back[5].astype(jnp.float32))
    grad_key_raw, grad_gain_k = key_back(grad_keys)
    grad_query_low = grad_query_raw.astype(jnp.bfloat16)
    grad_key_low = grad_key_raw.astype(jnp.bfloat16)
    part_query = outer_sum(normed, grad_query_low)
    part_key = outer_sum(normed, grad_key_low)
    part_value = outer_sum(normed, grad_value_low)
    grad_normed = (
        times_transposed(grad_query_low, attn_back[1])
        + times_transposed(grad_key_low, attn_back[2])
        + times_transposed(grad_value_low, attn_back[3])
    )
    _, input_back = jax.vjp(rms_scale, inputs, attn_back[0].astype(jnp.float32))
    grad_inputs_part, grad_gain_in = input_back(grad_normed)
    grad_tokens = grad_middle + grad_inputs_part
    everything = (
        lax.psum_scatter(grad_gain_in, "fsdp", scatter_dimension=0, tiled=True),
        lax.psum_scatter(part_query, "fsdp", scatter_dimension=0, tiled=True),
        lax.psum_scatter(part_key, "fsdp", scatter_dimension=0, tiled=True),
        lax.psum_scatter(part_value, "fsdp", scatter_dimension=0, tiled=True),
        lax.psum_scatter(grad_gain_q, "fsdp", scatter_dimension=0, tiled=True),
        lax.psum_scatter(grad_gain_k, "fsdp", scatter_dimension=0, tiled=True),
        lax.psum_scatter(part_output, "fsdp", scatter_dimension=0, tiled=True),
        lax.psum_scatter(grad_gain_post, "fsdp", scatter_dimension=0, tiled=True),
        lax.psum_scatter(grad_gain_pre, "fsdp", scatter_dimension=0, tiled=True),
        lax.psum_scatter(part_gate, "fsdp", scatter_dimension=0, tiled=True),
        lax.psum_scatter(part_up, "fsdp", scatter_dimension=0, tiled=True),
        lax.psum_scatter(part_down, "fsdp", scatter_dimension=0, tiled=True),
        lax.psum_scatter(grad_gain_ffn, "fsdp", scatter_dimension=0, tiled=True),
    )
    attn_owned = tuple(everything[:8])
    ffn_owned = tuple(everything[8:])
    return (result, grad_tokens) + tuple(attn_owned) + tuple(ffn_owned)


def solution(mesh):
    placed = (
        P("fsdp", None),
        P("fsdp", None),
        P("fsdp"),
        P("fsdp"),
        P("fsdp"),
        P("fsdp", None),
        P("fsdp", None),
        P("fsdp", None),
        P("fsdp"),
        P("fsdp"),
        P("fsdp", None),
        P("fsdp"),
        P("fsdp"),
        P("fsdp", None),
        P("fsdp", None),
        P("fsdp", None),
        P("fsdp"),
    )
    return jax.shard_map(
        on_device,
        mesh=mesh,
        in_specs=placed,
        out_specs=(
            P("fsdp", None),
            P("fsdp", None),
            P("fsdp"),
            P("fsdp", None),
            P("fsdp", None),
            P("fsdp", None),
            P("fsdp"),
            P("fsdp"),
            P("fsdp", None),
            P("fsdp"),
            P("fsdp"),
            P("fsdp", None),
            P("fsdp", None),
            P("fsdp", None),
            P("fsdp"),
        ),
        check_vma=False,
    )
```

profile of v0, /device:TPU:9, one launch (start us, length us, event | category | flops | bytes accessed | tf_op | source)
XLA Modules:
  0.0 856.5 jit_solution(1151008460264439427)
XLA Ops:
  15.7 40.3 %all-reduce.27 = (bf16[640]{0:T(1024)(128)(2,1)S(1)}, bf16[256]{0:T(256)(128)(2,1)S(1)}, bf16[256]{0:T(256)(128)(2,1)S(1)}, bf16[640]{0:T(1024)(128)(2,1)S(1)}, ...) all-reduce(bf16[640]{0:T(1024)(128)(2,1)S(1)} %dynamic-update-slice, ...), channel_id=1, replica_groups=mesh['fsdp'=32] {'fsdp'}, use_global_device_ids=true, to_apply=%add.4 | all-reduce | flops 3072 | bytes 12288
  58.7 35.9 %all-gather.1 = bf16[32,20,256]{2,1,0:T(8,128)(2,1)S(1)} all-gather(bf16[1,20,256]{2,1,0:T(8,128)(2,1)S(1)} %bitcast.115), channel_id=1, replica_groups=mesh['fsdp'=32] {'fsdp'}, dimensions={0}, use_global_device_ids=true | all-gather | bytes 337920 | tf_op jit(solution)/shard_map/all_gather | solution.py:139
  94.7 38.3 %all-gather = bf16[32,20,256]{2,1,0:T(8,128)(2,1)S(1)} all-gather(bf16[1,20,256]{2,1,0:T(8,128)(2,1)S(1)} %bitcast.116), channel_id=1, replica_groups=mesh['fsdp'=32] {'fsdp'}, dimensions={0}, use_global_device_ids=true | all-gather | bytes 337920 | tf_op jit(solution)/shard_map/all_gather | solution.py:140
  140.9 3.1 multiply_cosine_fusion
  145.7 2.7 copy.114
  148.4 3.3 reshape.259
  151.7 5.3 multiply_reduce_fusion.2
  156.9 5.4 copy.108
  162.4 2.6 multiply_multiply_fusion.3
  166.0 7.7 fusion.9
  173.8 9.0 %fusion.8 = f32[4,1024]{1,0:T(4,128)S(1)} fusion(f32[1024,1024,4]{1,0,2:T(8,128)} %get-tuple-element.137, f32[4,1024]{1,0:T(4,128)S(1)} %get-tuple-element.136, pred[1024,1024]{0,1:T(8,128)(4,1)S(1)} %copy.107), kind=kLoop, calls=%fused_computation.9 | loop fusion | flops 12578816 | bytes 17858560 | tf_op jit(solution)/shard_map/reduce_sum | solution.py:89
  182.8 9.5 %fusion.39 = bf16[256,4,1024]{2,0,1:T(8,128)(2,1)} fusion(bf16[1024,256,1]{1,0,2:T(8,128)(2,1)S(1)} %copy-done.35, f32[1024,1024,4]{1,0,2:T(8,128)} %get-tuple-element.137, f32[4,1024]{1,0:T(4,128)S(1)} %fusion.8, f32[4,1024]{1,0:T(4,128)S(1)} %get-tuple-element.136, pred[1024,1024]{0,1:T(8,128)(4,1)S(1)} %copy.107), kind=kOutput, calls=%fused_computation.81 | convolution fusion | flops 2165309440 | bytes 20480000 | tf_op jit(solution)/shard_map/htu,ud->thd/dot_general | solution.py:91
  192.3 3.7 multiply_reduce_fusion.11
  198.9 5.2 reshape.261
  204.1 40.0 %all-gather.19.cloned.1.call-done = bf16[32,20,2048]{2,1,0:T(8,128)(2,1)} async-done(((bf16[1,20,2048]{2,1,0:T(8,128)(2,1)}), bf16[32,20,2048]{2,1,0:T(8,128)(2,1)}) %all-gather.19.cloned.1.call-update) | async-done | bytes 2621456 | tf_op jit(solution)/shard_map/all_gather | solution.py:176
  244.1 5.2 reshape.263
  249.4 5.8 fusion.95
  255.2 3.3 copy-done.95
  258.4 8.9 %multiply_convert_fusion.1 = (bf16[1024,2048]{1,0:T(8,128)(2,1)}, f32[1024,2048]{1,0:T(8,128)}) fusion(f32[1024,2048]{1,0:T(8,128)S(1)} %fusion.95, bf16[1024,640]{0,1:T(8,128)(2,1)S(1)} %copy-done.31, bf16[640,2048]{1,0:T(8,128)(2,1)S(1)} %copy-done.21), kind=kOutput, calls=%fused_computation.24 | convolution fusion | flops 2705326080 | bytes 24903680 | tf_op jit(solution)/shard_map/dot_general | solution.py:11
  267.3 36.1 %all-gather.13.cloned.1.call-done = bf16[2048,640]{1,0:T(8,128)(2,1)} async-done(((bf16[64,640]{1,0:T(8,128)(2,1)}), bf16[2048,640]{1,0:T(8,128)(2,1)}) %all-gather.13.cloned.1.call-update) | async-done | bytes 2621456 | tf_op jit(solution)/shard_map/all_gather | solution.py:177
  303.4 5.7 multiply_reduce_fusion.9
  310.7 2.4 fusion.32
  314.0 12.7 %multiply_convert_fusion = (bf16[1024,2048]{1,0:T(8,128)(2,1)}, bf16[1024,2048]{1,0:T(8,128)(2,1)}) fusion(f32[1024,2048]{1,0:T(8,128)S(1)} %copy-done.96, f32[1024,2048]{1,0:T(8,128)} %get-tuple-element.141, bf16[1024,640]{0,1:T(8,128)(2,1)S(1)} %get-tuple-element.120, bf16[2048,640]{1,0:T(8,128)(2,1)S(1)} %copy-done.93), kind=kOutput, calls=%fused_computation.23 | convolution fusion | flops 2734686208 | bytes 29097984 | tf_op jit(solution)/shard_map/dot_general | solution.py:15
  326.7 5.1 fusion.96
  331.8 4.0 multiply_reduce_fusion.4
  335.8 2.2 multiply_reduce_fusion.5
  340.5 3.3 fusion.98
  343.9 3.2 convolution_convert_fusion
  347.1 12.4 %fusion.5 = (f32[4,1024]{1,0:T(4,128)S(1)}, f32[1024,1024,4]{1,0,2:T(8,128)}) fusion(f32[1024,1024,4]{1,0,2:T(8,128)} %get-tuple-element.137, f32[4,1024]{1,0:T(4,128)S(1)} %log_add_fusion, pred[1024,1024]{0,1:T(8,128)(4,1)S(1)} %copy-done.5, bf16[1024,256,1]{1,0,2:T(8,128)(2,1)S(1)} %copy-done.35, bf16[1024,4,256]{0,2,1:T(8,128)(2,1)S(1)} %bitcast.107), kind=kOutput, calls=%fused_computation.2 | convolution fusion | flops 2164256768 | bytes 37257216 | tf_op jit(solution)/shard_map/thd,ud->htu/dot_general | solution.py:100
  359.5 12.2 %fusion.7 = bf16[4,1024,1024]{1,2,0:T(8,128)(2,1)S(1)} fusion(f32[1024,1024,4]{1,0,2:T(8,128)} %get-tuple-element.146, f32[1024,1024,4]{1,0,2:T(8,128)} %get-tuple-element.137, f32[4,1024]{1,0:T(4,128)S(1)} %get-tuple-element.145, f32[4,1024]{1,0:T(4,128)S(1)} %log_add_fusion, pred[1024,1024]{0,1:T(8,128)(4,1)S(1)} %copy-done.5), kind=kLoop, calls=%fused_computation.4 | loop fusion | flops 20971520 | bytes 43024384 | tf_op jit(solution)/shard_map/convert_element_type | solution.py:107
  371.8 5.6 multiply_bitcast_fusion
  378.4 5.2 fusion.101
  384.9 2.9 multiply_add_fusion.1
  390.4 2.7 fusion.24
  393.1 4.4 copy.122
  397.5 7.0 convolution_bitcast_fusion
  408.4 9.4 %fusion.43 = bf16[1024,256]{1,0:T(8,128)(2,1)S(1)} fusion(bf16[1024,4,256]{0,2,1:T(8,128)(2,1)S(1)} %bitcast.108, f32[1024,1024,4]{1,0,2:T(8,128)} %get-tuple-element.137, f32[4,1024]{1,0:T(4,128)S(1)} %log_add_fusion, pred[1024,1024]{0,1:T(8,128)(4,1)S(1)} %copy-done.5), kind=kOutput, calls=%fused_computation.86 | convolution fusion | flops 2160328704 | bytes 20463616 | tf_op jit(solution)/shard_map/htu,thd->ud/dot_general | solution.py:103
  420.1 3.0 fusion.85
  423.1 4.5 fusion.100
  427.7 4.7 fusion.99
  432.3 246.9 %fusion.92 = (f32[24,1024]{1,0:T(8,128)S(1)}, f32[24,256]{1,0:T(8,128)S(1)}, f32[24,256]{1,0:T(8,128)S(1)}, f32[24,2048]{1,0:T(8,128)S(1)}, f32[24,2048]{1,0:T(8,128)S(1)}) fusion(f32[640,1024]{1,0:T(8,128)} %fusion.85, f32[640,256]{1,0:T(8,128)} %fusion.83, f32[640,256]{1,0:T(8,128)S(1)} %fusion.81, f32[640,2048]{1,0:T(8,128)} %fusion.99, ...), kind=kCustom, calls=%all-reduce-scatter.5 | all-reduce-scatter fusion | flops 4325377 | bytes 14958592
  679.3 4.1 collective-permute-start.10
  683.4 2.4 collective-permute-start.9
  687.8 8.9 %collective-permute-start.11 = (f32[4,256]{1,0:T(4,128)S(1)}, f32[4,256]{1,0:T(4,128)S(1)}, u32[]{:S(2)}, u32[]{:S(2)}) collective-permute-start(f32[4,256]{1,0:T(4,128)S(1)} %slice.21), channel_id=1, source_target_pairs={{0,6},{1,7},{2,8},{3,9},{4,10},{5,11},{6,12},{7,13},{8,14},{9,15},... | collective-permute-start | bytes 12296
  698.8 3.5 fusion.102
  704.4 2.4 collective-permute-start.7
  706.9 3.4 collective-permute-start.6
  714.8 2.3 collective-permute-start.14
  717.2 3.1 collective-permute-start.13
  720.3 3.4 collective-permute-start.12
  737.3 3.4 collective-permute-start
  748.5 2.3 collective-permute-start.18
  750.9 2.2 fusion.35
  753.0 2.6 copy.129
  757.8 43.1 %all-reduce.26 = (f32[640]{0:T(1024)S(1)}, f32[256]{0:T(256)S(1)}, f32[256]{0:T(256)S(1)}, f32[640]{0:T(1024)S(1)}, f32[640]{0:T(1024)S(1)}, /*index=5*/f32[640]{0:T(1024)S(1)}) all-reduce(f32[640]{0:T(1024)S(1)} %copy-done.76, f32[256]{0:T(256)} %get-tuple-element.75, ...), channel_id=2, replica_groups=mesh['fsdp'=32] {'fsdp'}, use_global_device_ids=true, to_apply=%region_18.19.clone | all-reduce | flops 3072 | bytes 24576
  804.4 3.4 concatenate.10
  807.8 4.8 concatenate.11
  813.3 4.7 collective-permute-start.28
  818.0 3.7 collective-permute-start.27
  823.7 2.5 collective-permute-start.25
  826.2 3.4 collective-permute-start.24
  830.2 4.9 concatenate.9
  835.7 5.3 concatenate.12
  842.6 5.4 concatenate.13
  (342 shorter events, 84.3 us)
Async XLA Ops:
  7.2 141.2 %all-gather.15.cloned.1.call-start = ((), (), s32[]{:S(2)}) async-start(), calls=%async_computation.6 | async-start | bytes 1622016 | tf_op jit(solution)/shard_map/all_gather | solution.py:138
  7.9 184.4 %all-gather.11.cloned.1.call-start = ((), (), s32[]{:S(2)}) async-start(), calls=%async_computation.2 | async-start | bytes 1351680 | tf_op jit(solution)/shard_map/all_gather | solution.py:143
  8.7 190.3 %all-gather.17.cloned.1.call-start = ((), (), s32[]{:S(2)}) async-start(), calls=%async_computation.7 | async-start | bytes 3244032 | tf_op jit(solution)/shard_map/all_gather | solution.py:175
  9.4 234.7 %all-gather.19.cloned.1.call-start = ((), (), s32[]{:S(2)}) async-start(), calls=%async_computation.8 | async-start | bytes 3244032 | tf_op jit(solution)/shard_map/all_gather | solution.py:176
  10.0 293.5 %all-gather.13.cloned.1.call-start = ((), (), s32[]{:S(2)}) async-start(), calls=%async_computation.3 | async-start | bytes 2703360 | tf_op jit(solution)/shard_map/all_gather | solution.py:177
  10.6 838.9 %reduce-scatter.13.cloned.1.call-start = ((), (), s32[]{:S(2)}) async-start(), calls=%async_computation.4 | async-start | bytes 2703360 | tf_op jit(solution)/shard_map/reduce_scatter | solution.py:262
  10.6 130.3 %copy-start.91 = (f32[128]{0:T(128)}, f32[128]{0:T(128)S(1)}, u32[]{:S(2)}) copy-start(f32[128]{0:T(128)S(1)} %multiply_power_fusion) | copy-start | bytes 1540
  56.0 83.8 %copy-start.83 = (f32[256]{0:T(256)}, f32[256]{0:T(256)S(1)}, u32[]{:S(2)}) copy-start(f32[256]{0:T(256)S(1)} %convert_element_type.113) | copy-start | bytes 3076
  56.0 106.3 %copy-start.85 = (f32[256]{0:T(256)}, f32[256]{0:T(256)S(1)}, u32[]{:S(2)}) copy-start(f32[256]{0:T(256)S(1)} %convert_element_type.116) | copy-start | bytes 3076
  56.0 95.6 %copy-start.56 = (f32[640]{0:T(1024)}, f32[640]{0:T(1024)S(1)}, u32[]{:S(2)}) copy-start(f32[640]{0:T(1024)S(1)} %convert_element_type.110) | copy-start | bytes 7684
  56.8 37.9 %copy-start.82 = (bf16[20,256]{1,0:T(8,128)(2,1)S(1)}, bf16[20,256]{1,0:T(8,128)(2,1)}, u32[]{:S(2)}) copy-start(bf16[20,256]{1,0:T(8,128)(2,1)} %param.24) | copy-start | bytes 30724
  58.7 82.2 %copy-start.60 = (f32[1024]{0:T(1024)}, f32[1024]{0:T(1024)S(1)}, u32[]{:S(2)}) copy-start(f32[1024]{0:T(1024)S(1)} %convert_subtract_fusion) | copy-start | bytes 12292
  94.7 44.3 %copy-start.27 = (bf16[640,256]{1,0:T(8,128)(2,1)}, bf16[640,256]{1,0:T(8,128)(2,1)S(1)}, u32[]{:S(2)}) copy-start(bf16[640,256]{1,0:T(8,128)(2,1)S(1)} %reshape.257) | copy-start | bytes 983044
  135.1 47.7 %copy-start.4 = (pred[1024,1024]{0,1:T(8,128)(4,1)}, pred[1024,1024]{0,1:T(8,128)(4,1)S(1)}, u32[]{:S(2)}) copy-start(pred[1024,1024]{0,1:T(8,128)(4,1)S(1)} %copy.107) | copy-start | bytes 3145732
  137.1 14.6 %copy-start.1 = (bf16[1024,640]{0,1:T(8,128)(2,1)}, bf16[1024,640]{0,1:T(8,128)(2,1)S(1)}, u32[]{:S(2)}) copy-start(bf16[1024,640]{0,1:T(8,128)(2,1)S(1)} %copy.106) | copy-start | bytes 3932164
  137.4 14.2 %copy-start.58 = (f32[1024]{0:T(1024)}, f32[1024]{0:T(1024)S(1)}, u32[]{:S(2)}) copy-start(f32[1024]{0:T(1024)S(1)} %fusion.67) | copy-start | bytes 12292
  144.2 20.7 %copy-start.17 = (f32[1024,128]{1,0:T(8,128)}, f32[1024,128]{1,0:T(8,128)S(1)}, u32[]{:S(2)}) copy-start(f32[1024,128]{1,0:T(8,128)S(1)} %copy.109) | copy-start | bytes 1572868
  145.7 19.3 %copy-start.19 = (f32[1024,128]{1,0:T(8,128)}, f32[1024,128]{1,0:T(8,128)S(1)}, u32[]{:S(2)}) copy-start(f32[1024,128]{1,0:T(8,128)S(1)} %copy.110) | copy-start | bytes 1572868
  313.0 13.7 %copy-start.29 = (bf16[1024,640]{0,1:T(8,128)(2,1)}, bf16[1024,640]{0,1:T(8,128)(2,1)S(1)}, u32[]{:S(2)}) copy-start(bf16[1024,640]{0,1:T(8,128)(2,1)S(1)} %get-tuple-element.120) | copy-start | bytes 3932164
  314.0 12.7 %copy-start.23 = (bf16[640,2048]{1,0:T(8,128)(2,1)S(1)}, bf16[640,2048]{1,0:T(8,128)(2,1)}, u32[]{:S(2)}) copy-start(bf16[640,2048]{1,0:T(8,128)(2,1)} %reshape.261) | copy-start | bytes 7864324
  343.8 505.6 %reduce-scatter.15.cloned.1.call-start = ((), (), s32[]{:S(2)}) async-start(), calls=%async_computation.5 | async-start | bytes 5406720 | tf_op jit(solution)/shard_map/reduce_scatter | solution.py:267
  347.1 12.4 %copy-start.15 = (bf16[1024,1024]{0,1:T(8,128)(2,1)}, bf16[1024,1024]{0,1:T(8,128)(2,1)S(1)}, u32[]{:S(2)}) copy-start(bf16[1024,1024]{0,1:T(8,128)(2,1)S(1)} %convolution_convert_fusion) | copy-start | bytes 6291460
  679.3 31.1 %collective-permute-start.10 = (f32[24,256]{1,0:T(8,128)S(1)}, f32[24,256]{1,0:T(8,128)S(1)}, u32[]{:S(2)}, u32[]{:S(2)}) collective-permute-start(f32[24,256]{1,0:T(8,128)S(1)} %get-tuple-element.107), channel_id=1, source_target_pairs={{0,5},{1,6},{2,7},{3,8},{4,9},{5,10},{6,11},{7,12},{8,13},{9,14},{... | collective-permute-start | bytes 73736
  683.4 28.9 %collective-permute-start.9 = (f32[24,256]{1,0:T(8,128)S(1)}, f32[24,256]{1,0:T(8,128)S(1)}, u32[]{:S(2)}, u32[]{:S(2)}) collective-permute-start(f32[24,256]{1,0:T(8,128)S(1)} %get-tuple-element.107), channel_id=1, source_target_pairs={{0,4},{1,5},{2,6},{3,7},{4,8},{5,9},{6,10},{7,11},{8,12},{9,13},{1... | collective-permute-start | bytes 73736
  685.8 16.5 %collective-permute-start.17 = (f32[4,256]{1,0:T(4,128)S(1)}, f32[4,256]{1,0:T(4,128)S(1)}, u32[]{:S(2)}, u32[]{:S(2)}) collective-permute-start(f32[4,256]{1,0:T(4,128)S(1)} %slice.22), channel_id=1, source_target_pairs={{0,6},{1,7},{2,8},{3,9},{4,10},{5,11},{6,12},{7,13},{8,14},{9,15},... | collective-permute-start | bytes 12296
  687.8 16.6 %collective-permute-start.11 = (f32[4,256]{1,0:T(4,128)S(1)}, f32[4,256]{1,0:T(4,128)S(1)}, u32[]{:S(2)}, u32[]{:S(2)}) collective-permute-start(f32[4,256]{1,0:T(4,128)S(1)} %slice.21), channel_id=1, source_target_pairs={{0,6},{1,7},{2,8},{3,9},{4,10},{5,11},{6,12},{7,13},{8,14},{9,15},... | collective-permute-start | bytes 12296
  696.7 17.5 %copy-start.34 = (bf16[640,256]{1,0:T(8,128)(2,1)S(1)}, bf16[640,256]{1,0:T(8,128)(2,1)}, u32[]{:S(2)}) copy-start(bf16[640,256]{1,0:T(8,128)(2,1)} %copy-done.33) | copy-start | bytes 983044
  696.7 17.5 %copy-start.37 = (bf16[1024,256]{1,0:T(8,128)(2,1)S(1)}, bf16[1024,256]{1,0:T(8,128)(2,1)}, u32[]{:S(2)}) copy-start(bf16[1024,256]{1,0:T(8,128)(2,1)} %copy-done.36) | copy-start | bytes 1572868
  696.7 10.1 %collective-permute-start.5 = (f32[4,1024]{1,0:T(4,128)S(1)}, f32[4,1024]{1,0:T(4,128)}, u32[]{:S(2)}, u32[]{:S(2)}) collective-permute-start(f32[4,1024]{1,0:T(4,128)S(1)} %slice.20), channel_id=1, source_target_pairs={{0,6},{1,7},{2,8},{3,9},{4,10},{5,11},{6,12},{7,13},{8,14},{9,15},... | collective-permute-start | bytes 49160
  702.3 25.3 %copy-start.28 = (bf16[640,256]{1,0:T(8,128)(2,1)S(1)}, bf16[640,256]{1,0:T(8,128)(2,1)}, u32[]{:S(2)}) copy-start(bf16[640,256]{1,0:T(8,128)(2,1)} %copy-done.27) | copy-start | bytes 983044
  702.3 12.5 %collective-permute-start.8 = (f32[24,256]{1,0:T(8,128)S(1)}, f32[24,256]{1,0:T(8,128)S(1)}, u32[]{:S(2)}, u32[]{:S(2)}) collective-permute-start(f32[24,256]{1,0:T(8,128)S(1)} %get-tuple-element.107), channel_id=1, source_target_pairs={{0,3},{1,4},{2,5},{3,6},{4,7},{5,8},{6,9},{7,10},{8,11},{9,12},{10... | collective-permute-start | bytes 73736
  704.4 12.8 %collective-permute-start.7 = (f32[24,256]{1,0:T(8,128)S(1)}, f32[24,256]{1,0:T(8,128)S(1)}, u32[]{:S(2)}, u32[]{:S(2)}) collective-permute-start(f32[24,256]{1,0:T(8,128)S(1)} %get-tuple-element.107), channel_id=1, source_target_pairs={{0,2},{1,3},{2,4},{3,5},{4,6},{5,7},{6,8},{7,9},{8,10},{9,11},{10,... | collective-permute-start | bytes 73736
  706.9 13.4 %collective-permute-start.6 = (f32[24,256]{1,0:T(8,128)S(1)}, f32[24,256]{1,0:T(8,128)S(1)}, u32[]{:S(2)}, u32[]{:S(2)}) collective-permute-start(f32[24,256]{1,0:T(8,128)S(1)} %get-tuple-element.107), channel_id=1, source_target_pairs={{0,1},{1,2},{2,3},{3,4},{4,5},{5,6},{6,7},{7,8},{8,9},{9,10},{10,1... | collective-permute-start | bytes 73736
  710.3 13.4 %collective-permute-start.16 = (f32[24,256]{1,0:T(8,128)S(1)}, f32[24,256]{1,0:T(8,128)S(1)}, u32[]{:S(2)}, u32[]{:S(2)}) collective-permute-start(f32[24,256]{1,0:T(8,128)S(1)} %get-tuple-element.108), channel_id=1, source_target_pairs={{0,5},{1,6},{2,7},{3,8},{4,9},{5,10},{6,11},{7,12},{8,13},{9,14},{... | collective-permute-start | bytes 73736
  712.3 17.2 %copy-start.66 = (f32[24,256]{1,0:T(8,128)}, f32[24,256]{1,0:T(8,128)S(1)}, u32[]{:S(2)}) copy-start(f32[24,256]{1,0:T(8,128)S(1)} %collective-permute-done.9) | copy-start | bytes 73732
  712.3 13.4 %collective-permute-start.15 = (f32[24,256]{1,0:T(8,128)S(1)}, f32[24,256]{1,0:T(8,128)S(1)}, u32[]{:S(2)}, u32[]{:S(2)}) collective-permute-start(f32[24,256]{1,0:T(8,128)S(1)} %get-tuple-element.108), channel_id=1, source_target_pairs={{0,4},{1,5},{2,6},{3,7},{4,8},{5,9},{6,10},{7,11},{8,12},{9,13},{1... | collective-permute-start | bytes 73736
  714.8 25.9 %copy-start.63 = (f32[1024]{0:T(1024)S(1)}, f32[1024]{0:T(1024)}, u32[]{:S(2)}) copy-start(f32[1024]{0:T(1024)} %copy-done.62) | copy-start | bytes 12292
  714.8 36.1 %copy-start.7 = (f32[1024,640]{0,1:T(8,128)S(1)}, f32[1024,640]{0,1:T(8,128)}, u32[]{:S(2)}) copy-start(f32[1024,640]{0,1:T(8,128)} %copy-done.6) | copy-start | bytes 7864324
  714.8 14.6 %copy-start.68 = (f32[24,256]{1,0:T(8,128)}, f32[24,256]{1,0:T(8,128)S(1)}, u32[]{:S(2)}) copy-start(f32[24,256]{1,0:T(8,128)S(1)} %collective-permute-done.8) | copy-start | bytes 73732
  714.8 14.6 %collective-permute-start.14 = (f32[24,256]{1,0:T(8,128)S(1)}, f32[24,256]{1,0:T(8,128)S(1)}, u32[]{:S(2)}, u32[]{:S(2)}) collective-permute-start(f32[24,256]{1,0:T(8,128)S(1)} %get-tuple-element.108), channel_id=1, source_target_pairs={{0,3},{1,4},{2,5},{3,6},{4,7},{5,8},{6,9},{7,10},{8,11},{9,12},{10... | collective-permute-start | bytes 73736
  717.2 14.2 %collective-permute-start.13 = (f32[24,256]{1,0:T(8,128)S(1)}, f32[24,256]{1,0:T(8,128)S(1)}, u32[]{:S(2)}, u32[]{:S(2)}) collective-permute-start(f32[24,256]{1,0:T(8,128)S(1)} %get-tuple-element.108), channel_id=1, source_target_pairs={{0,2},{1,3},{2,4},{3,5},{4,6},{5,7},{6,8},{7,9},{8,10},{9,11},{10,... | collective-permute-start | bytes 73736
  720.3 13.0 %collective-permute-start.12 = (f32[24,256]{1,0:T(8,128)S(1)}, f32[24,256]{1,0:T(8,128)S(1)}, u32[]{:S(2)}, u32[]{:S(2)}) collective-permute-start(f32[24,256]{1,0:T(8,128)S(1)} %get-tuple-element.108), channel_id=1, source_target_pairs={{0,1},{1,2},{2,3},{3,4},{4,5},{5,6},{6,7},{7,8},{8,9},{9,10},{10,1... | collective-permute-start | bytes 73736
  723.7 11.6 %collective-permute-start.29 = (f32[4,2048]{1,0:T(4,128)S(1)}, f32[4,2048]{1,0:T(4,128)S(1)}, u32[]{:S(2)}, u32[]{:S(2)}) collective-permute-start(f32[4,2048]{1,0:T(4,128)S(1)} %slice.24), channel_id=1, source_target_pairs={{0,6},{1,7},{2,8},{3,9},{4,10},{5,11},{6,12},{7,13},{8,14},{9,15},... | collective-permute-start | bytes 98312
  725.7 11.6 %collective-permute-start.23 = (f32[4,2048]{1,0:T(4,128)S(1)}, f32[4,2048]{1,0:T(4,128)}, u32[]{:S(2)}, u32[]{:S(2)}) collective-permute-start(f32[4,2048]{1,0:T(4,128)S(1)} %slice.23), channel_id=1, source_target_pairs={{0,6},{1,7},{2,8},{3,9},{4,10},{5,11},{6,12},{7,13},{8,14},{9,15},... | collective-permute-start | bytes 98312
  729.5 21.3 %copy-start.73 = (f32[24,256]{1,0:T(8,128)}, f32[24,256]{1,0:T(8,128)S(1)}, u32[]{:S(2)}) copy-start(f32[24,256]{1,0:T(8,128)S(1)} %collective-permute-done.14) | copy-start | bytes 73732
  729.5 11.2 %collective-permute-start.4 = (f32[24,1024]{1,0:T(8,128)S(1)}, f32[24,1024]{1,0:T(8,128)S(1)}, u32[]{:S(2)}, u32[]{:S(2)}) collective-permute-start(f32[24,1024]{1,0:T(8,128)S(1)} %get-tuple-element.106), channel_id=1, source_target_pairs={{0,5},{1,6},{2,7},{3,8},{4,9},{5,10},{6,11},{7,12},{8,13},{9,14},{... | collective-permute-start | bytes 294920
  731.4 19.4 %copy-start.74 = (f32[24,256]{1,0:T(8,128)}, f32[24,256]{1,0:T(8,128)S(1)}, u32[]{:S(2)}) copy-start(f32[24,256]{1,0:T(8,128)S(1)} %collective-permute-done.13) | copy-start | bytes 73732
  731.4 11.2 %collective-permute-start.3 = (f32[24,1024]{1,0:T(8,128)S(1)}, f32[24,1024]{1,0:T(8,128)S(1)}, u32[]{:S(2)}, u32[]{:S(2)}) collective-permute-start(f32[24,1024]{1,0:T(8,128)S(1)} %get-tuple-element.106), channel_id=1, source_target_pairs={{0,4},{1,5},{2,6},{3,7},{4,8},{5,9},{6,10},{7,11},{8,12},{9,13},{1... | collective-permute-start | bytes 294920
  733.4 17.5 %copy-start.75 = (f32[24,256]{1,0:T(8,128)}, f32[24,256]{1,0:T(8,128)S(1)}, u32[]{:S(2)}) copy-start(f32[24,256]{1,0:T(8,128)S(1)} %collective-permute-done.12) | copy-start | bytes 73732
  733.4 11.2 %collective-permute-start.2 = (f32[24,1024]{1,0:T(8,128)S(1)}, f32[24,1024]{1,0:T(8,128)S(1)}, u32[]{:S(2)}, u32[]{:S(2)}) collective-permute-start(f32[24,1024]{1,0:T(8,128)S(1)} %get-tuple-element.106), channel_id=1, source_target_pairs={{0,3},{1,4},{2,5},{3,6},{4,7},{5,8},{6,9},{7,10},{8,11},{9,12},{10... | collective-permute-start | bytes 294920
  735.3 11.2 %collective-permute-start.1 = (f32[24,1024]{1,0:T(8,128)S(1)}, f32[24,1024]{1,0:T(8,128)S(1)}, u32[]{:S(2)}, u32[]{:S(2)}) collective-permute-start(f32[24,1024]{1,0:T(8,128)S(1)} %get-tuple-element.106), channel_id=1, source_target_pairs={{0,2},{1,3},{2,4},{3,5},{4,6},{5,7},{6,8},{7,9},{8,10},{9,11},{10,... | collective-permute-start | bytes 294920
  737.3 11.2 %collective-permute-start = (f32[24,1024]{1,0:T(8,128)S(1)}, f32[24,1024]{1,0:T(8,128)S(1)}, u32[]{:S(2)}, u32[]{:S(2)}) collective-permute-start(f32[24,1024]{1,0:T(8,128)S(1)} %get-tuple-element.106), channel_id=1, source_target_pairs={{0,1},{1,2},{2,3},{3,4},{4,5},{5,6},{6,7},{7,8},{8,9},{9,10},{10,1... | collective-permute-start | bytes 294920
  740.7 72.6 %collective-permute-start.22 = (f32[24,2048]{1,0:T(8,128)S(1)}, f32[24,2048]{1,0:T(8,128)S(1)}, u32[]{:S(2)}, u32[]{:S(2)}) collective-permute-start(f32[24,2048]{1,0:T(8,128)S(1)} %get-tuple-element.109), channel_id=1, source_target_pairs={{0,5},{1,6},{2,7},{3,8},{4,9},{5,10},{6,11},{7,12},{8,13},{9,14},{... | collective-permute-start | bytes 589832
  742.6 75.4 %collective-permute-start.21 = (f32[24,2048]{1,0:T(8,128)S(1)}, f32[24,2048]{1,0:T(8,128)}, u32[]{:S(2)}, u32[]{:S(2)}) collective-permute-start(f32[24,2048]{1,0:T(8,128)S(1)} %get-tuple-element.109), channel_id=1, source_target_pairs={{0,4},{1,5},{2,6},{3,7},{4,8},{5,9},{6,10},{7,11},{8,12},{9,13},{1... | collective-permute-start | bytes 589832
  744.6 77.1 %collective-permute-start.20 = (f32[24,2048]{1,0:T(8,128)S(1)}, f32[24,2048]{1,0:T(8,128)}, u32[]{:S(2)}, u32[]{:S(2)}) collective-permute-start(f32[24,2048]{1,0:T(8,128)S(1)} %get-tuple-element.109), channel_id=1, source_target_pairs={{0,3},{1,4},{2,5},{3,6},{4,7},{5,8},{6,9},{7,10},{8,11},{9,12},{10... | collective-permute-start | bytes 589832
  746.5 77.1 %collective-permute-start.19 = (f32[24,2048]{1,0:T(8,128)S(1)}, f32[24,2048]{1,0:T(8,128)}, u32[]{:S(2)}, u32[]{:S(2)}) collective-permute-start(f32[24,2048]{1,0:T(8,128)S(1)} %get-tuple-element.109), channel_id=1, source_target_pairs={{0,2},{1,3},{2,4},{3,5},{4,6},{5,7},{6,8},{7,9},{8,10},{9,11},{10,... | collective-permute-start | bytes 589832
  748.5 77.7 %collective-permute-start.18 = (f32[24,2048]{1,0:T(8,128)S(1)}, f32[24,2048]{1,0:T(8,128)}, u32[]{:S(2)}, u32[]{:S(2)}) collective-permute-start(f32[24,2048]{1,0:T(8,128)S(1)} %get-tuple-element.109), channel_id=1, source_target_pairs={{0,1},{1,2},{2,3},{3,4},{4,5},{5,6},{6,7},{7,8},{8,9},{9,10},{10,1... | collective-permute-start | bytes 589832
  755.6 48.8 %copy-start.67 = (f32[24,256]{1,0:T(8,128)S(1)}, f32[24,256]{1,0:T(8,128)}, u32[]{:S(2)}) copy-start(f32[24,256]{1,0:T(8,128)} %copy-done.66) | copy-start | bytes 73732
  757.7 84.9 %copy-start.65 = (f32[4,2048]{1,0:T(4,128)S(1)}, f32[4,2048]{1,0:T(4,128)}, u32[]{:S(2)}) copy-start(f32[4,2048]{1,0:T(4,128)} %copy-done.64) | copy-start | bytes 98308
  813.3 27.8 %collective-permute-start.28 = (f32[24,2048]{1,0:T(8,128)S(1)}, f32[24,2048]{1,0:T(8,128)S(1)}, u32[]{:S(2)}, u32[]{:S(2)}) collective-permute-start(f32[24,2048]{1,0:T(8,128)S(1)} %get-tuple-element.110), channel_id=1, source_target_pairs={{0,5},{1,6},{2,7},{3,8},{4,9},{5,10},{6,11},{7,12},{8,13},{9,14},{... | collective-permute-start | bytes 589832
  818.0 23.1 %collective-permute-start.27 = (f32[24,2048]{1,0:T(8,128)S(1)}, f32[24,2048]{1,0:T(8,128)S(1)}, u32[]{:S(2)}, u32[]{:S(2)}) collective-permute-start(f32[24,2048]{1,0:T(8,128)S(1)} %get-tuple-element.110), channel_id=1, source_target_pairs={{0,4},{1,5},{2,6},{3,7},{4,8},{5,9},{6,10},{7,11},{8,12},{9,13},{1... | collective-permute-start | bytes 589832
  821.7 19.4 %collective-permute-start.26 = (f32[24,2048]{1,0:T(8,128)S(1)}, f32[24,2048]{1,0:T(8,128)S(1)}, u32[]{:S(2)}, u32[]{:S(2)}) collective-permute-start(f32[24,2048]{1,0:T(8,128)S(1)} %get-tuple-element.110), channel_id=1, source_target_pairs={{0,3},{1,4},{2,5},{3,6},{4,7},{5,8},{6,9},{7,10},{8,11},{9,12},{10... | collective-permute-start | bytes 589832
  823.7 17.5 %collective-permute-start.25 = (f32[24,2048]{1,0:T(8,128)S(1)}, f32[24,2048]{1,0:T(8,128)S(1)}, u32[]{:S(2)}, u32[]{:S(2)}) collective-permute-start(f32[24,2048]{1,0:T(8,128)S(1)} %get-tuple-element.110), channel_id=1, source_target_pairs={{0,2},{1,3},{2,4},{3,5},{4,6},{5,7},{6,8},{7,9},{8,10},{9,11},{10,... | collective-permute-start | bytes 589832
  826.2 16.4 %collective-permute-start.24 = (f32[24,2048]{1,0:T(8,128)S(1)}, f32[24,2048]{1,0:T(8,128)}, u32[]{:S(2)}, u32[]{:S(2)}) collective-permute-start(f32[24,2048]{1,0:T(8,128)S(1)} %get-tuple-element.110), channel_id=1, source_target_pairs={{0,1},{1,2},{2,3},{3,4},{4,5},{5,6},{6,7},{7,8},{8,9},{9,10},{10,1... | collective-permute-start | bytes 589832
  (74 other events, 331.7 us)
Sparse Core Ops, SparseCore 0:
  10.9 55.6 all-gather.14
  69.5 53.7 all-gather.10
  126.2 57.4 all-gather.16
  186.4 57.7 all-gather.18
  246.8 56.5 all-gather.12
  343.9 126.1 reduce-scatter.12
  473.0 161.8 reduce-scatter.14
where the time goes:
time: 865 us; the launch traced here: 856 us
  blocking collectives  405 us (47%)
  matrix products  138 us (16%)
  local copies, waits for them, and re-layouts  86 us (10%)
  starting transfers between devices  81.3 us (9%)
  waiting for transfers between devices  79.4 us (9%)
  other arithmetic  50.5 us (6%)
  between operations  16.2 us (2%)
    unnamed x3, blocking collectives  330 us
    unnamed x30, starting transfers between devices  81.1 us
    unnamed x244, local copies, waits for them, and re-layouts  72.6 us
    all_gather x1, waiting for transfers between devices, on_device(): lax.all_gather(w_up, 'fsdp', axis=0, tiled=True)  40 us
    all_gather x1, blocking collectives, on_device(): lax.all_gather(w_value, 'fsdp', axis=0, tiled=True)  38.3 us
    all_gather x1, waiting for transfers between devices, on_device(): lax.all_gather(w_down, 'fsdp', axis=0, tiled=True)  36.1 us
    all_gather x1, blocking collectives, on_device(): lax.all_gather(w_key, 'fsdp', axis=0, tiled=True)  35.9 us
    dot_general x7, matrix products, product(): return jnp.dot(left_side, right_side, preferred_element_type=jnp.float32)  31.5 us
  transfers between devices with their start and end apart: 37, of which 2 were waited for; matrix products, arithmetic and copies ran while one was open for 55% of the time, Pallas kernels for 0%

commit v1 on v0

v1 whole, which is shorter than its diff:
```python
import jax
import jax.numpy as jnp
from jax import lax
from jax.sharding import PartitionSpec as P

AX = "fsdp"
epsilon = 1e-06
rope_base = 1000000.0
BF = jnp.bfloat16
F32 = jnp.float32
LANES = 128


def product(left_side, right_side):
    return jnp.dot(left_side, right_side, preferred_element_type=jnp.float32)


def times_transposed(left_side, right_side):
    return lax.dot_general(
        left_side, right_side, (((1,), (1,)), ((), ())), preferred_element_type=jnp.float32
    )


def outer_sum(left_side, right_side):
    return lax.dot_general(
        left_side, right_side, (((0,), (0,)), ((), ())), preferred_element_type=jnp.float32
    )


def rms_scale(vector_rows, gain_row):
    return (
        vector_rows
        * lax.rsqrt(jnp.mean(vector_rows * vector_rows, axis=-1, keepdims=True) + epsilon)
        * gain_row
    )


def rotate(vector_rows, positions):
    half_width = vector_rows.shape[-1] // 2
    frequency = rope_base ** (
        -2.0 * jnp.arange(half_width, dtype=jnp.float32) / vector_rows.shape[-1]
    )
    angles = positions[:, None] * frequency[None, :]
    if vector_rows.ndim == 3:
        angles = angles[:, None, :]
    cosine = jnp.cos(angles)
    sine_part = jnp.sin(angles)
    first_half = vector_rows[..., :half_width]
    second_half = vector_rows[..., half_width:]
    return jnp.concatenate(
        [
            first_half * cosine - second_half * sine_part,
            second_half * cosine + first_half * sine_part,
        ],
        axis=-1,
    )


def prep_query(raw_rows, gain_row, positions):
    shaped = raw_rows.reshape(raw_rows.shape[0], -1, gain_row.shape[0])
    return rotate(rms_scale(shaped, gain_row), positions) * 0.0625


def prep_key(raw_rows, gain_row, positions):
    return rotate(rms_scale(raw_rows, gain_row), positions)


def glu_mix(gating, upward):
    return jax.nn.gelu(gating, approximate=True) * upward


def layout(lengths, starts, slot_count):
    slot_index = jnp.arange(slot_count, dtype=jnp.int32)
    inside = (slot_index[None, :] >= starts[:, None]) & (
        slot_index[None, :] < starts[:, None] + lengths[:, None]
    )
    member = inside.astype(jnp.float32)
    live_mask = jnp.sum(member, axis=0)
    offset = jnp.sum(member * starts[:, None].astype(jnp.float32), axis=0)
    positions = slot_index.astype(jnp.float32) - offset
    same_seq = jnp.dot(member.T, member, preferred_element_type=jnp.float32) > 0.5
    allowed = same_seq & (slot_index[None, :] <= slot_index[:, None]) | (
        slot_index[None, :] == slot_index[:, None]
    )
    return (live_mask, positions, allowed)


def attend(queries, key_rows, value_rows, allowed):
    scores = jnp.einsum("thd,ud->htu", queries, key_rows, preferred_element_type=jnp.float32)
    masked = jnp.where(allowed[None], scores, -1e30)
    row_peak = jnp.max(masked, axis=-1, keepdims=True)
    exponent = jnp.exp(masked - row_peak)
    row_total = jnp.sum(exponent, axis=-1, keepdims=True)
    probability = (exponent / row_total).astype(jnp.bfloat16)
    mixture = jnp.einsum("htu,ud->thd", probability, value_rows, preferred_element_type=jnp.float32)
    return (mixture, row_peak + jnp.log(row_total))


def attend_back(queries, key_rows, value_rows, allowed, log_total, grad_mixture):
    scores = jnp.einsum("thd,ud->htu", queries, key_rows, preferred_element_type=jnp.float32)
    masked = jnp.where(allowed[None], scores, -1e30)
    probability = jnp.exp(masked - log_total)
    weights_low = probability.astype(jnp.bfloat16)
    grad_probs = jnp.einsum(
        "thd,ud->htu", grad_mixture, value_rows, preferred_element_type=jnp.float32
    )
    grad_values = jnp.einsum(
        "htu,thd->ud", weights_low, grad_mixture, preferred_element_type=jnp.float32
    )
    row_inner = jnp.sum(probability * grad_probs, axis=-1, keepdims=True)
    grad_scores = (probability * (grad_probs - row_inner)).astype(jnp.bfloat16)
    grad_queries = jnp.einsum(
        "htu,ud->thd", grad_scores, key_rows, preferred_element_type=jnp.float32
    )
    grad_keys = jnp.einsum("htu,thd->ud", grad_scores, queries, preferred_element_type=jnp.float32)
    return (grad_queries, grad_keys, grad_values)


class Mover:
    def __init__(self, device_count):
        self.n = device_count
        self.chips = device_count // 2
        self.digits = 0
        while 4 ** (self.digits + 1) <= self.chips:
            self.digits += 1
        self.me = lax.axis_index(AX)
        self.core = self.me % 2
        self.chip = self.me // 2

    def swap(self, value, mask=1):
        return lax.ppermute(value, AX, [(i, i ^ mask) for i in range(self.n)])

    def in_core_order(self, mine, other):
        first = self.core == 0
        return jnp.where(first, mine, other), jnp.where(first, other, mine)

    def gather(self, narrow, tall, gains):
        rows = narrow[0].shape[0]
        halves = [jnp.split(w, 2, axis=1) for w in narrow]
        low = jnp.concatenate([h[0] for h in halves], axis=1)
        high = jnp.concatenate([h[1] for h in halves], axis=1)
        first = self.core == 0
        mine = jnp.where(first, low, high)
        other = self.swap(jnp.where(first, high, low))
        both = jnp.concatenate(self.in_core_order(mine, other), axis=0)
        tiles = both.reshape(2 * rows, -1, LANES).transpose(1, 0, 2).reshape(-1, LANES)
        parts = [tiles]
        for w in tall:
            parts.append(w.reshape(w.shape[0], -1, LANES).transpose(1, 0, 2).reshape(-1, LANES))
        if gains:
            flat = jnp.concatenate(gains)
            parts.append(jnp.pad(flat, (0, 8 * LANES - flat.shape[0])).reshape(8, LANES))
        whole = lax.all_gather(jnp.concatenate(parts, axis=0), AX, axis=0)
        whole = whole.reshape(self.chips, 2, -1, LANES)
        at = 0
        out_narrow, out_tall, out_gains = [], [], []
        for w in narrow:
            t = w.shape[1] // (2 * LANES)
            piece = whole[:, :, at : at + t * 2 * rows].reshape(self.chips, 2, t, 2 * rows, LANES)
            out_narrow.append(piece.transpose(0, 3, 1, 2, 4).reshape(self.n * rows, w.shape[1]))
            at += t * 2 * rows
        for w in tall:
            t = w.shape[1] // LANES
            piece = whole[:, :, at : at + t * w.shape[0]].reshape(self.n, t, w.shape[0], LANES)
            out_tall.append(piece.transpose(0, 2, 1, 3).reshape(self.n * w.shape[0], w.shape[1]))
            at += t * w.shape[0]
        if gains:
            piece = whole[:, :, at:].reshape(self.n, 8 * LANES)
            start = 0
            for g in gains:
                out_gains.append(piece[:, start : start + g.shape[0]].reshape(-1).astype(F32))
                start += g.shape[0]
        return out_narrow, out_tall, out_gains

    def reduce(self, narrow, tall, gains):
        parts = []
        for g in narrow:
            rows = g.shape[0] // self.chips
            t = g.shape[1] // (2 * LANES)
            piece = g.astype(BF).reshape(self.chips, rows, 2, t, LANES).transpose(2, 0, 3, 1, 4)
            parts.append(piece.reshape(2, self.chips, t * rows, LANES))
        for g in tall:
            rows = g.shape[0] // self.n
            t = g.shape[1] // LANES
            piece = g.astype(BF).reshape(self.chips, 2, rows, t, LANES).transpose(1, 0, 3, 2, 4)
            parts.append(piece.reshape(2, self.chips, t * rows, LANES))
        if gains:
            flat = jnp.concatenate([g.reshape(self.n, -1) for g in gains], axis=1).astype(BF)
            flat = jnp.pad(flat, ((0, 0), (0, 8 * LANES - flat.shape[1])))
            parts.append(flat.reshape(self.chips, 2, 8, LANES).transpose(1, 0, 2, 3))
        packed = jnp.concatenate(parts, axis=2)
        keep = lax.dynamic_index_in_dim(packed, self.core, 0, keepdims=False)
        send = lax.dynamic_index_in_dim(packed, 1 - self.core, 0, keepdims=False)
        total = keep.astype(F32) + self.swap(send).astype(F32)
        for digit in range(self.digits):
            low = total.astype(BF).reshape(total.shape[0] // 4, 4, -1, LANES)
            here = (self.chip >> (2 * digit)) % 4
            moved = [
                self.swap(
                    lax.dynamic_index_in_dim(low, here ^ j, 1, keepdims=False),
                    j << (2 * digit + 1),
                )
                for j in (1, 2, 3)
            ]
            total = lax.dynamic_index_in_dim(
                total.reshape(low.shape), here, 1, keepdims=False
            )
            for m in moved:
                total = total + m.astype(F32)
        total = total[0]
        at = 0
        outs = []
        count = sum(g.shape[0] // self.chips * (g.shape[1] // (2 * LANES)) for g in narrow)
        if narrow:
            rows = narrow[0].shape[0] // self.n
            tiles = total[:count].reshape(-1, 2, rows, LANES)
            mine = lax.dynamic_index_in_dim(tiles, self.core, 1, keepdims=False)
            other = self.swap(lax.dynamic_index_in_dim(tiles, 1 - self.core, 1, keepdims=False))
            halves = self.in_core_order(mine, other)
            for g in narrow:
                t = g.shape[1] // (2 * LANES)
                both = jnp.stack([h[at : at + t] for h in halves])
                outs.append(both.transpose(2, 0, 1, 3).reshape(rows, g.shape[1]))
                at += t
        at = count
        for g in tall:
            rows = g.shape[0] // self.n
            t = g.shape[1] // LANES
            outs.append(
                total[at : at + t * rows].reshape(t, rows, LANES).transpose(1, 0, 2).reshape(rows, -1)
            )
            at += t * rows
        if gains:
            flat = total[at:].reshape(-1)
            start = 0
            for g in gains:
                own = g.shape[0] // self.n
                outs.append(flat[start : start + own])
                start += own
        return outs


def on_device(
    device_count,
    tokens,
    cotangent,
    seq_lens,
    seq_starts,
    input_gain,
    w_query,
    w_key,
    w_value,
    query_gain,
    key_gain,
    w_output,
    attn_post_gain,
    ffn_pre_gain,
    w_gate,
    w_up,
    w_down,
    ffn_post_gain,
):
    mover = Mover(device_count)
    slot_count = tokens.shape[0]
    live_mask, positions, allowed = layout(seq_lens, seq_starts, slot_count)
    (query_w, key_w, value_w), _, gains = mover.gather(
        [w_query, w_key, w_value],
        [],
        [input_gain, query_gain, key_gain, attn_post_gain, ffn_pre_gain, ffn_post_gain],
    )
    gain_in, gain_q, gain_k, gain_post, gain_pre, gain_ffn = gains
    (gate_w, up_w), (output_w, down_w), _ = mover.gather([w_gate, w_up], [w_output, w_down], [])
    head_count = query_w.shape[1] // key_w.shape[1]

    def query_piece(raw_rows, gain_row):
        return prep_query(raw_rows, gain_row, positions)

    def key_piece(raw_rows, gain_row):
        return prep_key(raw_rows, gain_row, positions)

    inputs = tokens.astype(jnp.float32)
    normed = rms_scale(inputs, gain_in).astype(jnp.bfloat16)
    query_raw = product(normed, query_w)
    key_raw = product(normed, key_w)
    value_low = product(normed, value_w).astype(jnp.bfloat16)
    query_low = query_piece(query_raw, gain_q).astype(jnp.bfloat16)
    key_low = key_piece(key_raw, gain_k).astype(jnp.bfloat16)
    mixture, log_total = attend(query_low, key_low, value_low, allowed)
    mixed_low = mixture.reshape(slot_count, -1).astype(jnp.bfloat16)
    attn_out = product(mixed_low, output_w)
    middle = inputs + rms_scale(attn_out, gain_post)
    normed_ffn = rms_scale(middle, gain_pre).astype(jnp.bfloat16)
    gating = product(normed_ffn, gate_w)
    upward = product(normed_ffn, up_w)
    active = glu_mix(gating, upward).astype(jnp.bfloat16)
    down_out = product(active, down_w)
    output_rows = middle + rms_scale(down_out, gain_ffn)
    result = (live_mask[:, None] * output_rows).astype(jnp.bfloat16)
    grad_output = cotangent.astype(jnp.float32) * live_mask[:, None]
    _, post_ffn_back = jax.vjp(rms_scale, down_out, gain_ffn)
    grad_down_out, grad_gain_ffn = post_ffn_back(grad_output)
    grad_down_low = grad_down_out.astype(jnp.bfloat16)
    grad_active = times_transposed(grad_down_low, down_w)
    part_down = outer_sum(active, grad_down_low)
    _, glu_back = jax.vjp(glu_mix, gating, upward)
    grad_gating, grad_upward = glu_back(grad_active)
    grad_gate_low = grad_gating.astype(jnp.bfloat16)
    grad_up_low = grad_upward.astype(jnp.bfloat16)
    part_gate = outer_sum(normed_ffn, grad_gate_low)
    part_up = outer_sum(normed_ffn, grad_up_low)
    grad_normed_ffn = times_transposed(grad_gate_low, gate_w) + times_transposed(grad_up_low, up_w)
    _, pre_ffn_back = jax.vjp(rms_scale, middle, gain_pre)
    grad_middle_part, grad_gain_pre = pre_ffn_back(grad_normed_ffn)
    grad_middle = grad_output + grad_middle_part
    _, post_attn_back = jax.vjp(rms_scale, attn_out, gain_post)
    grad_attn_out, grad_gain_post = post_attn_back(grad_middle)
    grad_attn_low = grad_attn_out.astype(jnp.bfloat16)
    part_output = outer_sum(mixed_low, grad_attn_low)
    own_gate, own_up, own_output, own_down = mover.reduce(
        [part_gate, part_up], [part_output, part_down], []
    )
    grad_mixture = (
        times_transposed(grad_attn_low, output_w)
        .astype(jnp.bfloat16)
        .reshape(slot_count, head_count, -1)
    )
    grad_queries, grad_keys, grad_values = attend_back(
        query_low, key_low, value_low, allowed, log_total, grad_mixture
    )
    grad_value_low = grad_values.astype(jnp.bfloat16)
    _, query_back = jax.vjp(query_piece, query_raw, gain_q)
    grad_query_raw, grad_gain_q = query_back(grad_queries)
    _, key_back = jax.vjp(key_piece, key_raw, gain_k)
    grad_key_raw, grad_gain_k = key_back(grad_keys)
    grad_query_low = grad_query_raw.astype(jnp.bfloat16)
    grad_key_low = grad_key_raw.astype(jnp.bfloat16)
    part_query = outer_sum(normed, grad_query_low)
    part_key = outer_sum(normed, grad_key_low)
    part_value = outer_sum(normed, grad_value_low)
    grad_normed = (
        times_transposed(grad_query_low, query_w)
        + times_transposed(grad_key_low, key_w)
        + times_transposed(grad_value_low, value_w)
    )
    _, input_back = jax.vjp(rms_scale, inputs, gain_in)
    grad_inputs_part, grad_gain_in = input_back(grad_normed)
    grad_tokens = grad_middle + grad_inputs_part
    (own_query, own_key, own_value, own_gin, own_gq, own_gk, own_gpost, own_gpre, own_gffn) = (
        mover.reduce(
            [part_query, part_key, part_value],
            [],
            [grad_gain_in, grad_gain_q, grad_gain_k, grad_gain_post, grad_gain_pre, grad_gain_ffn],
        )
    )
    return (
        result,
        grad_tokens,
        own_gin,
        own_query,
        own_key,
        own_value,
        own_gq,
        own_gk,
        own_output,
        own_gpost,
        own_gpre,
        own_gate,
        own_up,
        own_down,
        own_gffn,
    )


def solution(mesh):
    rows, flat = P(AX, None), P(AX)
    device_count = mesh.shape[AX]

    def block(*arrays):
        return on_device(device_count, *arrays)

    return jax.shard_map(
        block,
        mesh=mesh,
        in_specs=(
            rows, rows, flat, flat, flat, rows, rows, rows, flat, flat, rows, flat, flat, rows, rows, rows, flat,
        ),
        out_specs=(
            rows, rows, flat, rows, rows, rows, flat, flat, rows, flat, flat, rows, rows, rows, flat,
        ),
        check_vma=False,
    )
```

time: 865 us -> 502 us (0.58)
  blocking collectives: 405 us -> 0 us
  waiting for transfers between devices: 79.4 us -> 167 us
  starting transfers between devices: 81.3 us -> 16.7 us
  local copies, waits for them, and re-layouts: 86 us -> 112 us
  matrix products: 138 us -> 118 us
  other arithmetic: 50.5 us -> 62.2 us
    unnamed x3 -> x0, blocking collectives: 330 us -> none
    ppermute x0 -> x18, waiting for transfers between devices: none -> 85.6 us  [swap(): return lax.ppermute(value, AX, [(i, i ^ mask) for i in range(self.n)])]
    unnamed x30 -> x0, starting transfers between devices: 81.1 us -> none
    all_gather x2 -> x0, blocking collectives: 74.2 us -> none  [the longest x1 38.3 us: on_device(): lax.all_gather(w_value, 'fsdp', axis=0, tiled=True)]
    unnamed x244 -> x184, local copies, waits for them, and re-layouts: 72.6 us -> 25.7 us
    reshape x1 -> x30, local copies, waits for them, and re-layouts: 5.39 us -> 39.5 us  [the longest x3 14 us: gather(): piece.transpose(0, 3, 1, 2, 4).reshape(self.n * rows, w.shape[1])]
    transpose x0 -> x17, local copies, waits for them, and re-layouts: none -> 19.3 us  [the longest x6 9.16 us: gather(): piece.transpose(0, 3, 1, 2, 4).reshape(self.n * rows, w.shape[1])]
    ppermute x0 -> x18, starting transfers between devices: none -> 16.6 us  [swap(): return lax.ppermute(value, AX, [(i, i ^ mask) for i in range(self.n)])]
  transfers between devices with their start and end apart: 37 -> 20, of which waited for: 2 -> 11; matrix products, arithmetic and copies ran while one was open for 55% -> 23% of each run, Pallas kernels for 0% -> 0%
where the time goes in v1:
time: 502 us; the launch traced here: 492 us
  waiting for transfers between devices  167 us (33%)
  matrix products  118 us (24%)
  local copies, waits for them, and re-layouts  112 us (22%)
  other arithmetic  62.2 us (12%)
  starting transfers between devices  16.7 us (3%)
  between operations  16.1 us (3%)
    ppermute x18, waiting for transfers between devices, swap(): return lax.ppermute(value, AX, [(i, i ^ mask) for i in range(self.n)])  85.6 us
    all_gather x2, waiting for transfers between devices, gather(): whole = lax.all_gather(jnp.concatenate(parts, axis=0), AX, axis=0)  80.9 us
    dot_general x7, matrix products, times_transposed(): lax.dot_general(left_side, right_side, (((1,), (1,)), ((), ())), preferre...  26.8 us
    unnamed x184, local copies, waits for them, and re-layouts  25.7 us
    dot_general x7, matrix products, outer_sum(): lax.dot_general(left_side, right_side, (((0,), (0,)), ((), ())), preferre...  24.3 us
    dot_general x7, matrix products, product(): return jnp.dot(left_side, right_side, preferred_element_type=jnp.float32)  22.1 us
    ppermute x18, starting transfers between devices, swap(): return lax.ppermute(value, AX, [(i, i ^ mask) for i in range(self.n)])  16.6 us
    reshape x3, local copies, waits for them, and re-layouts, gather(): piece.transpose(0, 3, 1, 2, 4).reshape(self.n * rows, w.shape[1])  14 us
  transfers between devices with their start and end apart: 20, of which 11 were waited for; matrix products, arithmetic and copies ran while one was open for 23% of the time, Pallas kernels for 0%

profile of v1, /device:TPU:9, one launch (start us, length us, event | category | flops | bytes accessed | tf_op | source)
XLA Modules:
  0.0 491.7 jit_solution(4273778916565101962)
XLA Ops:
  9.6 4.1 concatenate.47
  20.3 2.0 copy.247
  22.3 2.9 copy.263
  25.6 45.6 %all-gather.5.cloned.1.call-done = bf16[7936,128]{1,0:T(8,128)(2,1)} async-done(((bf16[248,128]{1,0:T(8,128)(2,1)}), bf16[7936,128]{1,0:T(8,128)(2,1)}) %all-gather.5.cloned.1.call-update) | async-done | bytes 2031632 | tf_op jit(solution)/shard_map/all_gather | solution.py:153
  75.1 3.5 reshape.528
  78.5 2.4 copy.250
  84.8 1.9 multiply_reduce_fusion.2
  87.6 2.1 multiply_cosine_fusion
  91.6 7.8 %fusion.4 = (f32[4,1024]{1,0:T(4,128)S(1)}, f32[1024,1024,4]{1,0,2:T(8,128)}) fusion(pred[1024,1024]{0,1:T(8,128)(4,1)S(1)} %copy.247, f32[1024,4,128]{0,2,1:T(8,128)S(1)} %get-tuple-element.138, f32[1024,4,128]{0,2,1:T(8,128)S(1)} %get-tuple-element.137, bf16[1024,128]{0,1:T(8,128)(2,1)S(1)} %get-tuple-element.195, ...), kind=kOutput, calls=%fused_computation.10 | convolution fusion | flops 2160062464 | bytes 22560768 | tf_op jit(solution)/shard_map/thd,ud->htu/dot_general | solution.py:89
  99.5 9.1 %fusion.3 = f32[4,1024]{1,0:T(4,128)S(1)} fusion(f32[1024,1024,4]{1,0,2:T(8,128)} %get-tuple-element.210, f32[4,1024]{1,0:T(4,128)S(1)} %get-tuple-element.209, pred[1024,1024]{0,1:T(8,128)(4,1)S(1)} %copy.247), kind=kLoop, calls=%fused_computation.9 | loop fusion | flops 12578816 | bytes 17858560 | tf_op jit(solution)/shard_map/reduce_sum | solution.py:93
  110.0 9.7 %fusion.40 = bf16[256,4,1024]{2,0,1:T(8,128)(2,1)} fusion(bf16[1024,256,1]{1,0,2:T(8,128)(2,1)S(1)} %fusion.56, f32[1024,1024,4]{1,0,2:T(8,128)} %get-tuple-element.210, f32[4,1024]{1,0:T(4,128)S(1)} %fusion.3, f32[4,1024]{1,0:T(4,128)S(1)} %get-tuple-element.209, pred[1024,1024]{0,1:T(8,128)(4,1)S(1)} %copy.247), kind=kOutput, calls=%fused_computation.96 | convolution fusion | flops 2165309440 | bytes 20480000 | tf_op jit(solution)/shard_map/htu,ud->thd/dot_general | solution.py:95
  119.7 35.3 %all-gather.7.cloned.1.call-done = bf16[35840,128]{1,0:T(8,128)(2,1)} async-done(((bf16[1120,128]{1,0:T(8,128)(2,1)}), bf16[35840,128]{1,0:T(8,128)(2,1)}) %all-gather.7.cloned.1.call-update) | async-done | bytes 9175056 | tf_op jit(solution)/shard_map/all_gather | solution.py:153
  156.4 5.2 %fusion.118 = (bf16[16,2,320,128]{3,2,1,0:T(8,128)(2,1)}, bf16[16,2,320,128]{3,2,1,0:T(8,128)(2,1)}, bf16[16,2,320,128]{3,2,1,0:T(8,128)(2,1)S(1)}) fusion(bf16[16,2,1120,128]{3,2,1,0:T(8,128)(2,1)} %bitcast.364), kind=kLoop, calls=%fused_computation.269 | loop fusion | bytes 15728640 | tf_op jit(solution)/shard_map/slice | solution.py:164
  166.4 2.0 copy.260
  168.4 5.2 %reshape.539 = bf16[640,2048]{1,0:T(8,128)(2,1)} reshape(bf16[16,40,2,8,128]{4,3,2,1,0:T(8,128)(2,1)} %copy.260) | data formatting | bytes 5242880 | tf_op jit(solution)/shard_map/reshape | solution.py:160
  173.6 3.8 copy.261
  177.4 5.3 %reshape.541 = bf16[640,2048]{1,0:T(8,128)(2,1)} reshape(bf16[16,40,2,8,128]{4,3,2,1,0:T(8,128)(2,1)} %copy.261) | data formatting | bytes 5242880 | tf_op jit(solution)/shard_map/reshape | solution.py:160
  182.8 4.2 copy.262
  188.7 3.5 fusion.127
  192.2 8.5 %multiply_convert_fusion.1 = (bf16[1024,2048]{1,0:T(8,128)(2,1)}, f32[1024,2048]{1,0:T(8,128)}) fusion(f32[1024,2048]{1,0:T(8,128)S(1)} %fusion.127, bf16[1024,640]{0,1:T(8,128)(2,1)S(1)} %multiply_convert_fusion.3, bf16[640,2048]{1,0:T(8,128)(2,1)S(1)} %copy-done.25), kind=kOutput, calls=%fused_computation.26 | convolution fusion | flops 2705326080 | bytes 24903680 | tf_op jit(solution)/shard_map/dot_general | solution.py:15
  200.7 5.1 %multiply_reduce_fusion.9 = (f32[1024]{0:T(1024)S(1)}, f32[1024,640]{0,1:T(8,128)S(1)}) fusion(bf16[1024,2048]{1,0:T(8,128)(2,1)} %get-tuple-element.213, bf16[256,8,5,128]{3,2,1,0:T(8,128)(2,1)S(1)} %bitcast.373), kind=kOutput, calls=%fused_computation.82 | convolution fusion | flops 2685664256 | bytes 9441280 | tf_op jit(solution)/shard_map/dot_general | solution.py:15
  206.8 2.3 fusion.27
  209.2 4.8 convolution_convert_fusion
  214.0 14.0 %multiply_convert_fusion = (bf16[1024,2048]{1,0:T(8,128)(2,1)}, bf16[1024,2048]{1,0:T(8,128)(2,1)}) fusion(f32[1024,2048]{1,0:T(8,128)} %copy-done.75, f32[1024,2048]{1,0:T(8,128)} %get-tuple-element.214, bf16[1024,640]{0,1:T(8,128)(2,1)S(1)} %get-tuple-element.142, bf16[256,8,5,128]{3,2,1,0:T(8,128)(2,1)S(1)} %bitcast.374), kind=kOutput, calls=%fused_computation.25 | convolution fusion | flops 2734686208 | bytes 29097984 | tf_op jit(solution)/shard_map/dot_general | solution.py:19
  228.0 6.5 %fusion.41 = bf16[80,8,16,128]{3,1,2,0:T(8,128)(2,1)} fusion(bf16[1024,640]{0,1:T(8,128)(2,1)S(1)} %multiply_convert_fusion.3, bf16[1024,2048]{1,0:T(8,128)(2,1)} %get-tuple-element.131), kind=kOutput, calls=%fused_computation.97 | convolution fusion | flops 2685665280 | bytes 8126464 | tf_op jit(solution)/shard_map/dot_general | solution.py:25
  234.5 2.9 fusion.128
  237.4 4.6 fusion.42
  242.0 3.4 multiply_reduce_fusion.4
  247.5 2.0 copy-done.74
  249.5 2.9 convolution_convert_fusion.4
  252.5 1.8 convolution_convert_fusion.3
  254.3 12.4 %fusion = (f32[4,1024]{1,0:T(4,128)S(1)}, f32[1024,1024,4]{1,0,2:T(8,128)}) fusion(f32[1024,1024,4]{1,0,2:T(8,128)} %get-tuple-element.210, f32[4,1024]{1,0:T(4,128)S(1)} %copy-done.41, pred[1024,1024]{0,1:T(8,128)(4,1)S(1)} %copy-done.7, bf16[1024,256,1]{1,0,2:T(8,128)(2,1)S(1)} %copy-done.43, bf16[1024,4,256]{0,2,1:T(8,128)(2,1)S(1)} %bitcast.371), kind=kOutput, calls=%fused_computation.2 | convolution fusion | flops 2164256768 | bytes 37257216 | tf_op jit(solution)/shard_map/thd,ud->htu/dot_general | solution.py:104
  266.7 12.7 %fusion.2 = bf16[4,1024,1024]{1,2,0:T(8,128)(2,1)S(1)} fusion(f32[1024,1024,4]{1,0,2:T(8,128)} %get-tuple-element.219, f32[1024,1024,4]{1,0,2:T(8,128)} %get-tuple-element.210, f32[4,1024]{1,0:T(4,128)S(1)} %get-tuple-element.218, f32[4,1024]{1,0:T(4,128)S(1)} %copy-done.41, pred[1024,1024]{0,1:T(8,128)(4,1)S(1)} %copy-done.7), kind=kLoop, calls=%fused_computation.4 | loop fusion | flops 20971520 | bytes 43024384 | tf_op jit(solution)/shard_map/convert_element_type | solution.py:111
  279.5 3.4 convolution_bitcast_fusion
  282.9 4.5 multiply_bitcast_fusion
  287.4 6.0 %fusion.53 = bf16[1024,256]{1,0:T(8,128)(2,1)} fusion(bf16[1024,4,256]{0,2,1:T(8,128)(2,1)} %bitcast.372, f32[1024,1024,4]{1,0,2:T(8,128)S(1)} %bitcast.351, f32[4,1024]{1,0:T(4,128)} %log_add_fusion, pred[1024,1024]{0,1:T(8,128)(4,1)S(1)} %copy-done.7), kind=kOutput, calls=%fused_computation.112 | convolution fusion | flops 2160328704 | bytes 20463616 | tf_op jit(solution)/shard_map/htu,thd->ud/dot_general | solution.py:107
  293.4 7.0 %reshape.571 = bf16[16,2,64,5,128]{4,3,2,1,0:T(8,128)(2,1)} reshape(bf16[2048,640]{1,0:T(8,128)(2,1)} %convolution_convert_fusion) | data formatting | bytes 5242880 | tf_op jit(solution)/shard_map/reshape | solution.py:185
  300.4 3.1 copy.286
  304.4 2.2 copy.283
  307.4 2.1 copy.284
  309.6 4.1 reshape.569
  313.7 2.0 copy.285
  316.0 3.0 pad_maximum_fusion
  319.1 2.4 dynamic-slice_bitcast_fusion
  321.5 2.5 copy-done.2
  324.2 2.1 fusion.72
  335.9 2.7 fusion.26
  340.9 4.3 convolution_convert_fusion.5
  345.2 3.1 reshape.545
  353.2 2.7 collective-permute-done.2
  355.9 2.8 fusion.116
  361.5 4.8 collective-permute-done.3
  367.1 5.6 %collective-permute-done.5 = bf16[4,248,128]{2,1,0:T(8,128)(2,1)S(1)} collective-permute-done((bf16[4,248,128]{2,1,0:T(8,128)(2,1)S(1)}, bf16[4,248,128]{2,1,0:T(8,128)(2,1)S(1)}, u32[]{:S(2)}, u32[]{:S(2)}) %collective-permute-start.5) | collective-permute-done | bytes 253984 | tf_op jit(solution)/shard_map/ppermute | solution.py:131
  376.6 4.7 fusion.30
  381.3 3.3 copy.294
  386.2 2.2 collective-permute-start.9
  388.3 7.4 %fusion.113 = (bf16[16,1120,128]{2,1,0:T(8,128)(2,1)}, f32[16,1120,128]{2,1,0:T(8,128)S(1)}) fusion(bf16[16,1120,128]{2,1,0:T(8,128)(2,1)} %collective-permute-done.10, bf16[2,16,1120,128]{3,2,1,0:T(8,128)(2,1)} %copy-done.2, s32[]{:T(128)S(6)} %select_n.160), kind=kLoop, calls=%fused_computation.266 | loop fusion | flops 9175040 | bytes 22937604 | tf_op jit(solution)/shard_map/convert_element_type | solution.py:196
  395.7 2.2 dynamic-slice_bitcast_fusion.3
  401.8 23.0 %collective-permute-done.11 = bf16[4,1120,128]{2,1,0:T(8,128)(2,1)S(1)} collective-permute-done((bf16[4,1120,128]{2,1,0:T(8,128)(2,1)S(1)}, bf16[4,1120,128]{2,1,0:T(8,128)(2,1)S(1)}, u32[]{:S(2)}, u32[]{:S(2)}) %collective-permute-start.11) | collective-permute-done | bytes 1146912 | tf_op jit(solution)/shard_map/ppermute | solution.py:131
  424.8 24.7 %collective-permute-done.13 = bf16[4,1120,128]{2,1,0:T(8,128)(2,1)S(1)} collective-permute-done((bf16[4,1120,128]{2,1,0:T(8,128)(2,1)S(1)}, bf16[4,1120,128]{2,1,0:T(8,128)(2,1)S(1)}, u32[]{:S(2)}, u32[]{:S(2)}) %collective-permute-start.13) | collective-permute-done | bytes 1146912 | tf_op jit(solution)/shard_map/ppermute | solution.py:131
  452.8 8.6 %collective-permute-done.14 = bf16[1,1120,128]{2,1,0:T(8,128)(2,1)S(1)} collective-permute-done((bf16[1,1120,128]{2,1,0:T(8,128)(2,1)S(1)}, bf16[1,1120,128]{2,1,0:T(8,128)(2,1)S(1)}, u32[]{:S(2)}, u32[]{:S(2)}) %collective-permute-start.14) | collective-permute-done | bytes 286752 | tf_op jit(solution)/shard_map/ppermute | solution.py:131
  461.5 2.6 collective-permute-done.15
  464.1 12.8 %collective-permute-done.16 = bf16[1,1120,128]{2,1,0:T(8,128)(2,1)S(1)} collective-permute-done((bf16[1,1120,128]{2,1,0:T(8,128)(2,1)S(1)}, bf16[1,1120,128]{2,1,0:T(8,128)(2,1)S(1)}, u32[]{:S(2)}, u32[]{:S(2)}) %collective-permute-start.16) | collective-permute-done | bytes 286752 | tf_op jit(solution)/shard_map/ppermute | solution.py:131
  477.2 2.3 collective-permute-start.17
  (338 shorter events, 71.9 us)
Async XLA Ops:
  7.2 11.3 %copy-start.36 = (bf16[1024,640]{1,0:T(8,128)(2,1)S(1)}, bf16[1024,640]{1,0:T(8,128)(2,1)}, u32[]{:S(2)}) copy-start(bf16[1024,640]{1,0:T(8,128)(2,1)} %param.17) | copy-start | bytes 3932164
  7.2 64.0 %all-gather.5.cloned.1.call-start = ((), (), s32[]{:S(2)}) async-start(), calls=%async_computation | async-start | bytes 2095104 | tf_op jit(solution)/shard_map/all_gather | solution.py:153
  8.9 4.8 collective-permute-start
  14.5 140.4 %all-gather.7.cloned.1.call-start = ((), (), s32[]{:S(2)}) async-start(), calls=%async_computation.1 | async-start | bytes 9461760 | tf_op jit(solution)/shard_map/all_gather | solution.py:153
  15.5 2.0 collective-permute-start.1
  19.2 90.0 %copy-start.3 = (bf16[1024,640]{0,1:T(8,128)(2,1)}, bf16[1024,640]{0,1:T(8,128)(2,1)S(1)}, u32[]{:S(2)}) copy-start(bf16[1024,640]{0,1:T(8,128)(2,1)S(1)} %copy.244) | copy-start | bytes 3932164
  22.2 87.7 %copy-start.6 = (pred[1024,1024]{0,1:T(8,128)(4,1)}, pred[1024,1024]{0,1:T(8,128)(4,1)S(1)}, u32[]{:S(2)}) copy-start(pred[1024,1024]{0,1:T(8,128)(4,1)S(1)} %copy.247) | copy-start | bytes 3145732
  25.1 62.5 %copy-start.70 = (f32[128]{0:T(128)}, f32[128]{0:T(128)S(1)}, u32[]{:S(2)}) copy-start(f32[128]{0:T(128)S(1)} %multiply_power_fusion) | copy-start | bytes 1540
  25.5 49.5 %copy-start.61 = (f32[1024]{0:T(1024)}, f32[1024]{0:T(1024)S(1)}, u32[]{:S(2)}) copy-start(f32[1024]{0:T(1024)S(1)} %fusion.31) | copy-start | bytes 12292
  25.5 83.6 %copy-start.57 = (f32[1024]{0:T(1024)}, f32[1024]{0:T(1024)S(1)}, u32[]{:S(2)}) copy-start(f32[1024]{0:T(1024)S(1)} %fusion.91) | copy-start | bytes 12292
  25.6 62.0 %copy-start.59 = (f32[1024]{0:T(1024)}, f32[1024]{0:T(1024)S(1)}, u32[]{:S(2)}) copy-start(f32[1024]{0:T(1024)S(1)} %convert_subtract_fusion) | copy-start | bytes 12292
  81.2 28.0 %copy-start.55 = (f32[640]{0:T(1024)}, f32[640]{0:T(1024)S(1)}, u32[]{:S(2)}) copy-start(f32[640]{0:T(1024)S(1)} %reshape.582) | copy-start | bytes 7684
  81.3 8.5 %copy-start.67 = (f32[256]{0:T(256)}, f32[256]{0:T(256)S(1)}, u32[]{:S(2)}) copy-start(f32[256]{0:T(256)S(1)} %reshape.584) | copy-start | bytes 3076
  82.8 4.0 copy-start.34
  82.9 4.0 copy-start.63
  83.1 26.0 %copy-start.38 = (bf16[16,40,2,1,128]{4,2,1,0,3:T(2,128)(2,1)}, bf16[16,40,2,1,128]{4,2,1,0,3:T(2,128)(2,1)S(1)}, u32[]{:S(2)}) copy-start(bf16[16,40,2,1,128]{4,2,1,0,3:T(2,128)(2,1)S(1)} %copy.246) | copy-start | bytes 983044
  86.8 4.0 copy-start
  86.8 4.0 copy-start.45
  91.6 7.9 %copy-start.29 = (f32[1024,4,128]{0,2,1:T(8,128)}, f32[1024,4,128]{0,2,1:T(8,128)S(1)}, u32[]{:S(2)}) copy-start(f32[1024,4,128]{0,2,1:T(8,128)S(1)} %get-tuple-element.137) | copy-start | bytes 6291460
  91.6 7.9 %copy-start.31 = (f32[1024,4,128]{0,2,1:T(8,128)}, f32[1024,4,128]{0,2,1:T(8,128)S(1)}, u32[]{:S(2)}) copy-start(f32[1024,4,128]{0,2,1:T(8,128)S(1)} %get-tuple-element.138) | copy-start | bytes 6291460
  110.0 9.7 %copy-start.42 = (bf16[1024,256,1]{1,0,2:T(8,128)(2,1)}, bf16[1024,256,1]{1,0,2:T(8,128)(2,1)S(1)}, u32[]{:S(2)}) copy-start(bf16[1024,256,1]{1,0,2:T(8,128)(2,1)S(1)} %fusion.56) | copy-start | bytes 1572868
  188.7 3.5 copy-start.25
  192.2 8.5 %copy-start.75 = (f32[1024,2048]{1,0:T(8,128)}, f32[1024,2048]{1,0:T(8,128)S(1)}, u32[]{:S(2)}) copy-start(f32[1024,2048]{1,0:T(8,128)S(1)} %fusion.127) | copy-start | bytes 25165828
  200.7 5.1 %copy-start.11 = (bf16[1024,640]{0,1:T(8,128)(2,1)S(1)}, bf16[1024,640]{0,1:T(8,128)(2,1)}, u32[]{:S(2)}) copy-start(bf16[1024,640]{0,1:T(8,128)(2,1)} %copy.263) | copy-start | bytes 3932164
  228.0 6.5 %copy-start.77 = (bf16[1024,2048]{1,0:T(8,128)(2,1)S(1)}, bf16[1024,2048]{1,0:T(8,128)(2,1)}, u32[]{:S(2)}) copy-start(bf16[1024,2048]{1,0:T(8,128)(2,1)} %get-tuple-element.131) | copy-start | bytes 12582916
  234.5 2.9 copy-start.76
  242.0 3.4 copy-start.10
  246.9 5.5 %copy-start.8 = (f32[1024,640]{0,1:T(8,128)}, f32[1024,640]{0,1:T(8,128)S(1)}, u32[]{:S(2)}) copy-start(f32[1024,640]{0,1:T(8,128)S(1)} %get-tuple-element.127) | copy-start | bytes 7864324
  249.5 2.9 copy-start.28
  254.3 12.5 %copy-start.17 = (bf16[1024,1024]{0,1:T(8,128)(2,1)}, bf16[1024,1024]{0,1:T(8,128)(2,1)S(1)}, u32[]{:S(2)}) copy-start(bf16[1024,1024]{0,1:T(8,128)(2,1)S(1)} %convolution_convert_fusion.3) | copy-start | bytes 6291460
  266.7 12.7 %copy-start.30 = (f32[1024,4,128]{0,2,1:T(8,128)S(1)}, f32[1024,4,128]{0,2,1:T(8,128)}, u32[]{:S(2)}) copy-start(f32[1024,4,128]{0,2,1:T(8,128)} %copy-done.29) | copy-start | bytes 6291460
  266.7 12.7 %copy-start.32 = (f32[1024,4,128]{0,2,1:T(8,128)S(1)}, f32[1024,4,128]{0,2,1:T(8,128)}, u32[]{:S(2)}) copy-start(f32[1024,4,128]{0,2,1:T(8,128)} %copy-done.31) | copy-start | bytes 6291460
  279.4 3.4 copy-start.48
  279.4 3.4 copy-start.50
  279.5 7.9 %slice-start = ((s8[16777216]{0:T(1024)(128)(4,1)}), s8[4194304]{0:T(1024)(128)(4,1)S(1)}, s32[]{:S(2)}) async-start(s8[16777216]{0:T(1024)(128)(4,1)} %bitcast.350), calls=%async_computation.2 | async-start | bytes 8388608
  279.5 7.9 %slice-start.1 = ((s8[16777216]{0:T(1024)(128)(4,1)}), s8[4194304]{0:T(1024)(128)(4,1)S(1)}, s32[]{:S(2)}) async-start(s8[16777216]{0:T(1024)(128)(4,1)} %bitcast.350), calls=%async_computation.3 | async-start | bytes 8388608
  282.9 4.5 slice-start.2
  282.9 4.5 slice-start.3
  300.4 3.1 copy-start.23
  319.0 5.0 %copy-start.2 = (bf16[2,16,1120,128]{3,2,1,0:T(8,128)(2,1)}, bf16[2,16,1120,128]{3,2,1,0:T(8,128)(2,1)S(1)}, u32[]{:S(2)}) copy-start(bf16[2,16,1120,128]{3,2,1,0:T(8,128)(2,1)S(1)} %pad_maximum_fusion) | copy-start | bytes 27525124
  319.0 5.2 %copy-start.40 = (f32[1024,256]{0,1:T(8,128)S(1)}, f32[1024,256]{0,1:T(8,128)}, u32[]{:S(2)}) copy-start(f32[1024,256]{0,1:T(8,128)} %convolution_bitcast_fusion) | copy-start | bytes 3145732
  319.0 5.2 %copy-start.60 = (f32[1024]{0:T(1024)S(1)}, f32[1024]{0:T(1024)}, u32[]{:S(2)}) copy-start(f32[1024]{0:T(1024)} %copy-done.59) | copy-start | bytes 12292
  319.0 5.2 %copy-start.71 = (f32[128]{0:T(128)S(1)}, f32[128]{0:T(128)}, u32[]{:S(2)}) copy-start(f32[128]{0:T(128)} %copy-done.70) | copy-start | bytes 1540
  319.0 7.3 %copy-start.52 = (f32[1024]{0:T(1024)S(1)}, f32[1024]{0:T(1024)}, u32[]{:S(2)}) copy-start(f32[1024]{0:T(1024)} %copy-done.51) | copy-start | bytes 12292
  319.1 7.3 %copy-start.64 = (f32[256]{0:T(256)S(1)}, f32[256]{0:T(256)}, u32[]{:S(2)}) copy-start(f32[256]{0:T(256)} %copy-done.63) | copy-start | bytes 3076
  324.0 64.4 %collective-permute-start.10 = (bf16[16,1120,128]{2,1,0:T(8,128)(2,1)}, bf16[16,1120,128]{2,1,0:T(8,128)(2,1)}, u32[]{:S(2)}, u32[]{:S(2)}) collective-permute-start(bf16[16,1120,128]{2,1,0:T(8,128)(2,1)} %dynamic-slice_bitcast_fusion), channel_id=1, source_target_pairs={{0,1},{1,0},{2,3},{3,2},{4,5},{5,4},{6,7},{7,6},{8,9},{9,8},{10,11... | collective-permute-start | bytes 13762568 | tf_op jit(solution)/shard_map/ppermute | solution.py:131
  324.2 2.8 copy-start.22
  352.9 3.0 collective-permute-start.2
  353.2 8.3 %copy-start.62 = (f32[1024]{0:T(1024)S(1)}, f32[1024]{0:T(1024)}, u32[]{:S(2)}) copy-start(f32[1024]{0:T(1024)} %copy-done.61) | copy-start | bytes 12292
  358.7 7.5 %collective-permute-start.3 = (bf16[4,248,128]{2,1,0:T(8,128)(2,1)S(1)}, bf16[4,248,128]{2,1,0:T(8,128)(2,1)S(1)}, u32[]{:S(2)}, u32[]{:S(2)}) collective-permute-start(bf16[4,248,128]{2,1,0:T(8,128)(2,1)S(1)} %get-tuple-element.153), channel_id=1, source_target_pairs={{0,2},{1,3},{2,0},{3,1},{4,6},{5,7},{6,4},{7,5},{8,10},{9,11},{10,... | collective-permute-start | bytes 761864 | tf_op jit(solution)/shard_map/ppermute | solution.py:131
  360.0 7.1 %collective-permute-start.4 = (bf16[4,248,128]{2,1,0:T(8,128)(2,1)S(1)}, bf16[4,248,128]{2,1,0:T(8,128)(2,1)S(1)}, u32[]{:S(2)}, u32[]{:S(2)}) collective-permute-start(bf16[4,248,128]{2,1,0:T(8,128)(2,1)S(1)} %get-tuple-element.155), channel_id=1, source_target_pairs={{0,4},{1,5},{2,6},{3,7},{4,0},{5,1},{6,2},{7,3},{8,12},{9,13},{10,... | collective-permute-start | bytes 761864 | tf_op jit(solution)/shard_map/ppermute | solution.py:131
  360.3 12.4 %collective-permute-start.5 = (bf16[4,248,128]{2,1,0:T(8,128)(2,1)S(1)}, bf16[4,248,128]{2,1,0:T(8,128)(2,1)S(1)}, u32[]{:S(2)}, u32[]{:S(2)}) collective-permute-start(bf16[4,248,128]{2,1,0:T(8,128)(2,1)S(1)} %get-tuple-element.154), channel_id=1, source_target_pairs={{0,6},{1,7},{2,4},{3,5},{4,2},{5,3},{6,0},{7,1},{8,14},{9,15},{10,... | collective-permute-start | bytes 761864 | tf_op jit(solution)/shard_map/ppermute | solution.py:131
  373.9 12.2 %collective-permute-start.6 = (bf16[1,248,128]{2,1,0:T(8,128)(2,1)S(1)}, bf16[1,248,128]{2,1,0:T(8,128)(2,1)S(1)}, u32[]{:S(2)}, u32[]{:S(2)}) collective-permute-start(bf16[1,248,128]{2,1,0:T(8,128)(2,1)S(1)} %get-tuple-element.162), channel_id=1, source_target_pairs={{0,8},{1,9},{2,10},{3,11},{4,12},{5,13},{6,14},{7,15},{8,0},{9,1},... | collective-permute-start | bytes 190472 | tf_op jit(solution)/shard_map/ppermute | solution.py:131
  374.2 11.9 %collective-permute-start.7 = (bf16[1,248,128]{2,1,0:T(8,128)(2,1)S(1)}, bf16[1,248,128]{2,1,0:T(8,128)(2,1)S(1)}, u32[]{:S(2)}, u32[]{:S(2)}) collective-permute-start(bf16[1,248,128]{2,1,0:T(8,128)(2,1)S(1)} %get-tuple-element.164), channel_id=1, source_target_pairs={{0,16},{1,17},{2,18},{3,19},{4,20},{5,21},{6,22},{7,23},{8,24},{9,... | collective-permute-start | bytes 190472 | tf_op jit(solution)/shard_map/ppermute | solution.py:131
  375.9 10.2 %collective-permute-start.8 = (bf16[1,248,128]{2,1,0:T(8,128)(2,1)S(1)}, bf16[1,248,128]{2,1,0:T(8,128)(2,1)S(1)}, u32[]{:S(2)}, u32[]{:S(2)}) collective-permute-start(bf16[1,248,128]{2,1,0:T(8,128)(2,1)S(1)} %get-tuple-element.163), channel_id=1, source_target_pairs={{0,24},{1,25},{2,26},{3,27},{4,28},{5,29},{6,30},{7,31},{8,16},{9,... | collective-permute-start | bytes 190472 | tf_op jit(solution)/shard_map/ppermute | solution.py:131
  381.3 3.3 copy-start.15
  386.2 15.6 %collective-permute-start.9 = (f32[6,20,128]{2,1,0:T(8,128)S(1)}, f32[6,20,128]{2,1,0:T(8,128)S(1)}, u32[]{:S(2)}, u32[]{:S(2)}) collective-permute-start(f32[6,20,128]{2,1,0:T(8,128)S(1)} %dynamic-slice_bitcast_fusion.8), channel_id=1, source_target_pairs={{0,1},{1,0},{2,3},{3,2},{4,5},{5,4},{6,7},{7,6},{8,9},{9,8},{10,11... | collective-permute-start | bytes 184328 | tf_op jit(solution)/shard_map/ppermute | solution.py:131
  397.9 26.9 %collective-permute-start.11 = (bf16[4,1120,128]{2,1,0:T(8,128)(2,1)S(1)}, bf16[4,1120,128]{2,1,0:T(8,128)(2,1)S(1)}, u32[]{:S(2)}, u32[]{:S(2)}) collective-permute-start(bf16[4,1120,128]{2,1,0:T(8,128)(2,1)S(1)} %get-tuple-element.139), channel_id=1, source_target_pairs={{0,2},{1,3},{2,0},{3,1},{4,6},{5,7},{6,4},{7,5},{8,10},{9,11},{10,... | collective-permute-start | bytes 3440648 | tf_op jit(solution)/shard_map/ppermute | solution.py:131
  398.3 26.5 %collective-permute-start.12 = (bf16[4,1120,128]{2,1,0:T(8,128)(2,1)S(1)}, bf16[4,1120,128]{2,1,0:T(8,128)(2,1)S(1)}, u32[]{:S(2)}, u32[]{:S(2)}) collective-permute-start(bf16[4,1120,128]{2,1,0:T(8,128)(2,1)S(1)} %get-tuple-element.141), channel_id=1, source_target_pairs={{0,4},{1,5},{2,6},{3,7},{4,0},{5,1},{6,2},{7,3},{8,12},{9,13},{10,... | collective-permute-start | bytes 3440648 | tf_op jit(solution)/shard_map/ppermute | solution.py:131
  399.5 50.0 %collective-permute-start.13 = (bf16[4,1120,128]{2,1,0:T(8,128)(2,1)S(1)}, bf16[4,1120,128]{2,1,0:T(8,128)(2,1)S(1)}, u32[]{:S(2)}, u32[]{:S(2)}) collective-permute-start(bf16[4,1120,128]{2,1,0:T(8,128)(2,1)S(1)} %get-tuple-element.140), channel_id=1, source_target_pairs={{0,6},{1,7},{2,4},{3,5},{4,2},{5,3},{6,0},{7,1},{8,14},{9,15},{10,... | collective-permute-start | bytes 3440648 | tf_op jit(solution)/shard_map/ppermute | solution.py:131
  450.1 11.3 %collective-permute-start.14 = (bf16[1,1120,128]{2,1,0:T(8,128)(2,1)S(1)}, bf16[1,1120,128]{2,1,0:T(8,128)(2,1)S(1)}, u32[]{:S(2)}, u32[]{:S(2)}) collective-permute-start(bf16[1,1120,128]{2,1,0:T(8,128)(2,1)S(1)} %get-tuple-element.146), channel_id=1, source_target_pairs={{0,8},{1,9},{2,10},{3,11},{4,12},{5,13},{6,14},{7,15},{8,0},{9,1},... | collective-permute-start | bytes 860168 | tf_op jit(solution)/shard_map/ppermute | solution.py:131
  451.3 12.8 %collective-permute-start.15 = (bf16[1,1120,128]{2,1,0:T(8,128)(2,1)S(1)}, bf16[1,1120,128]{2,1,0:T(8,128)(2,1)S(1)}, u32[]{:S(2)}, u32[]{:S(2)}) collective-permute-start(bf16[1,1120,128]{2,1,0:T(8,128)(2,1)S(1)} %get-tuple-element.148), channel_id=1, source_target_pairs={{0,16},{1,17},{2,18},{3,19},{4,20},{5,21},{6,22},{7,23},{8,24},{9,... | collective-permute-start | bytes 860168 | tf_op jit(solution)/shard_map/ppermute | solution.py:131
  452.1 24.8 %collective-permute-start.16 = (bf16[1,1120,128]{2,1,0:T(8,128)(2,1)S(1)}, bf16[1,1120,128]{2,1,0:T(8,128)(2,1)S(1)}, u32[]{:S(2)}, u32[]{:S(2)}) collective-permute-start(bf16[1,1120,128]{2,1,0:T(8,128)(2,1)S(1)} %get-tuple-element.147), channel_id=1, source_target_pairs={{0,24},{1,25},{2,26},{3,27},{4,28},{5,29},{6,30},{7,31},{8,16},{9,... | collective-permute-start | bytes 860168 | tf_op jit(solution)/shard_map/ppermute | solution.py:131
  477.2 5.6 %collective-permute-start.17 = (f32[16,20,128]{2,0,1:T(8,128)S(1)}, f32[16,20,128]{2,0,1:T(8,128)S(1)}, u32[]{:S(2)}, u32[]{:S(2)}) collective-permute-start(f32[16,20,128]{2,0,1:T(8,128)S(1)} %bitcast.411), channel_id=1, source_target_pairs={{0,1},{1,0},{2,3},{3,2},{4,5},{5,4},{6,7},{7,6},{8,9},{9,8},{10,11... | collective-permute-start | bytes 491528 | tf_op jit(solution)/shard_map/ppermute | solution.py:131
  (39 other events, 72.4 us)
Sparse Core Ops, SparseCore 0:
  14.7 56.4 all-gather.4
  74.6 80.3 all-gather.6

commit v2 on v1

v2 whole, which is shorter than its diff:
```python
import functools

import jax
import jax.numpy as jnp
from jax import lax
from jax.experimental import pallas as pl
from jax.experimental.pallas import tpu as pltpu
from jax.sharding import PartitionSpec as P

AX = "fsdp"
epsilon = 1e-06
rope_base = 1000000.0
BF = jnp.bfloat16
F32 = jnp.float32
LANES = 128
TILE = 256
STEP_ROWS = 80
GELU_C = 0.7978845608028654
GELU_K = 0.044715
BIG = -1e30


def mm(a, b):
    return lax.dot_general(a, b, (((1,), (0,)), ((), ())), preferred_element_type=F32)


def mm_bt(a, b):
    return lax.dot_general(a, b, (((1,), (1,)), ((), ())), preferred_element_type=F32)


def mm_at(a, b):
    return lax.dot_general(a, b, (((0,), (0,)), ((), ())), preferred_element_type=F32)


def row_mean(v):
    return jnp.mean(v, axis=-1, keepdims=True)


def fold_rows(v):
    return jnp.sum(v.reshape(v.shape[0] // 8, 8, v.shape[1]), axis=0)


def turn(v, cos, sin):
    half = v.shape[1] // 2
    a, b = v[:, :half], v[:, half:]
    return jnp.concatenate([a * cos - b * sin, b * cos + a * sin], axis=1)


def turn_back(v, cos, sin):
    half = v.shape[1] // 2
    a, b = v[:, :half], v[:, half:]
    return jnp.concatenate([a * cos + b * sin, b * cos - a * sin], axis=1)


def norm_back(du, unit, scale):
    return scale * (du - unit * row_mean(du * unit))


def slot_starts(slot, lens_ref, starts_ref):
    first = slot
    inside = jnp.zeros(slot.shape, F32)
    for s in range(lens_ref.shape[0]):
        member = (slot >= starts_ref[s]) & (slot < starts_ref[s] + lens_ref[s])
        first = jnp.where(member, starts_ref[s], first)
        inside = jnp.where(member, 1.0, inside)
    return first, inside


class Pack:
    def __init__(self, chips, narrow, tall, base):
        self.chips = chips
        self.base = base
        self.narrow = narrow
        self.tall = tall
        self.pair = narrow[0][0] // chips
        self.chips_per_step = STEP_ROWS // self.pair
        self.steps = chips // self.chips_per_step
        at = 0
        self.narrow_at = []
        for _, cols in narrow:
            self.narrow_at.append(at)
            at += cols // (2 * LANES) * self.pair
        self.tall_at = []
        for rows, cols in tall:
            self.tall_at.append(at)
            at += cols // LANES * (rows // (2 * chips))
        self.used = at

    def unpack(self, step, ref, narrow_refs, tall_refs):
        rows = slice(self.base, self.base + self.used)
        slabs = [[ref[j, p, rows, :].astype(F32) for p in range(2)] for j in range(self.chips_per_step)]
        at_row = pl.multiple_of(step * STEP_ROWS, 16)
        for (_, cols), start, out in zip(self.narrow, self.narrow_at, narrow_refs):
            tiles = cols // (2 * LANES)
            for p in range(2):
                for t in range(tiles):
                    lo = start + t * self.pair
                    value = jnp.concatenate([s[p][lo : lo + self.pair] for s in slabs], axis=0)
                    col = (p * tiles + t) * LANES
                    out[pl.ds(at_row, STEP_ROWS), col : col + LANES] = value.astype(BF)
        for (rows, cols), start, out in zip(self.tall, self.tall_at, tall_refs):
            own = rows // (2 * self.chips)
            group = self.chips_per_step * 2 * own
            at_tall = pl.multiple_of(step * group, 16)
            for t in range(cols // LANES):
                lo = start + t * own
                value = jnp.concatenate(
                    [s[p][lo : lo + own] for s in slabs for p in range(2)], axis=0
                )
                out[pl.ds(at_tall, group), t * LANES : (t + 1) * LANES] = value.astype(BF)

    def pack(self, step, core, narrow_refs, tall_refs, keep_ref, send_ref):
        at_row = pl.multiple_of(step * STEP_ROWS, 8)
        pieces = [[[] for _ in range(2)] for _ in range(self.chips_per_step)]
        for (_, cols), acc in zip(self.narrow, narrow_refs):
            tiles = cols // (2 * LANES)
            for p in range(2):
                for t in range(tiles):
                    col = (p * tiles + t) * LANES
                    value = acc[pl.ds(at_row, STEP_ROWS), col : col + LANES]
                    for j in range(self.chips_per_step):
                        pieces[j][p].append(value[j * self.pair : (j + 1) * self.pair])
        for (rows, cols), acc in zip(self.tall, tall_refs):
            own = rows // (2 * self.chips)
            group = self.chips_per_step * 2 * own
            at_tall = pl.multiple_of(step * group, 8)
            for t in range(cols // LANES):
                value = acc[pl.ds(at_tall, group), t * LANES : (t + 1) * LANES]
                for j in range(self.chips_per_step):
                    for p in range(2):
                        lo = (2 * j + p) * own
                        pieces[j][p].append(value[lo : lo + own])
        for j in range(self.chips_per_step):
            first = jnp.concatenate(pieces[j][0], axis=0)
            second = jnp.concatenate(pieces[j][1], axis=0)
            keep_ref[j] = jnp.where(core == 0, first, second).astype(BF)
            send_ref[j] = jnp.where(core == 0, second, first).astype(BF)


def forward_kernel(
    pack, heads,
    lens_ref, starts_ref, g_ref, x_ref, cos_ref, sin_ref, gin_ref, gq_ref, gk_ref,
    w_out, h1_ref, qraw_ref, kraw_ref, qn_ref, kn_ref, v_ref, ob_ref,
    w_s, k_s, v_s, bias_s,
):
    step = pl.program_id(0)
    hd = gk_ref.shape[1]
    model = x_ref.shape[1]
    wide = heads * hd

    @pl.when(step < pack.steps)
    def _():
        pack.unpack(step, g_ref, [w_s.at[:, :wide], w_s.at[:, wide : wide + hd], w_s.at[:, wide + hd :]], [])
        w_out[...] = w_s[pl.ds(pl.multiple_of(step * STEP_ROWS, 16), STEP_ROWS), :]

    tile = step - pack.steps

    @pl.when(tile >= 0)
    def _():
        x = x_ref[...].astype(F32)
        scale = lax.rsqrt(row_mean(x * x) + epsilon)
        h1 = (x * scale * gin_ref[...]).astype(BF)
        h1_ref[...] = h1
        cos, sin = cos_ref[...], sin_ref[...]
        raw = mm(h1, w_s[:, :wide])
        qraw_ref[...] = raw
        for h in range(heads):
            part = raw[:, h * hd : (h + 1) * hd]
            unit = part * lax.rsqrt(row_mean(part * part) + epsilon)
            qn_ref[:, h * hd : (h + 1) * hd] = (turn(unit * gq_ref[...], cos, sin) * 0.0625).astype(BF)
        kraw = mm(h1, w_s[:, wide : wide + hd])
        kraw_ref[...] = kraw
        unit = kraw * lax.rsqrt(row_mean(kraw * kraw) + epsilon)
        kn = turn(unit * gk_ref[...], cos, sin).astype(BF)
        kn_ref[...] = kn
        v = mm(h1, w_s[:, wide + hd :]).astype(BF)
        v_ref[...] = v
        at = pl.multiple_of(tile * TILE, TILE)
        k_s[pl.ds(at, TILE), :] = kn
        v_s[pl.ds(at, TILE), :] = v

    for c in range(k_s.shape[0] // TILE):

        @pl.when(tile == c)
        def _():
            span = (c + 1) * TILE
            slot = c * TILE + lax.broadcasted_iota(jnp.int32, (TILE, 1), 0)
            first, _ = slot_starts(slot, lens_ref, starts_ref)
            other = lax.broadcasted_iota(jnp.int32, (TILE, span), 1)
            bias_s[:, :span] = jnp.where((other >= first) & (other <= slot), 0.0, BIG)
            for h in range(heads):
                q = qn_ref[:, h * hd : (h + 1) * hd]
                s = mm_bt(q, k_s[:span, :]) + bias_s[:, :span]
                e = jnp.exp(s - jnp.max(s, axis=-1, keepdims=True))
                inv = 1.0 / jnp.sum(e, axis=-1, keepdims=True)
                o = mm((e * inv).astype(BF), v_s[:span, :])
                ob_ref[:, h * hd : (h + 1) * hd] = o.astype(BF)


def middle_kernel(
    pack, tiles,
    lens_ref, starts_ref, core_ref, g_ref, x_ref, ob_ref, ct_ref, gpost_ref, gpre_ref, gffn_ref,
    res_ref, dx1_ref, dob_ref, dgains_ref, keep_ref, send_ref,
    wg_s, wu_s, wo_s, wd_s, ag_s, au_s, ao_s, ad_s, gain_s,
):
    step = pl.program_id(0)

    @pl.when(step == 0)
    def _():
        for ref in (ag_s, au_s, ao_s, ad_s, gain_s):
            ref[...] = jnp.zeros(ref.shape, F32)

    @pl.when(step < pack.steps)
    def _():
        pack.unpack(step, g_ref, [wg_s, wu_s], [wo_s, wd_s])

    tile = step - pack.steps

    @pl.when((tile >= 0) & (tile < tiles))
    def _():
        slot = tile * TILE + lax.broadcasted_iota(jnp.int32, (TILE, 1), 0)
        _, live = slot_starts(slot, lens_ref, starts_ref)
        ob = ob_ref[...]
        attn = mm(ob, wo_s[...])
        r1 = lax.rsqrt(row_mean(attn * attn) + epsilon)
        na = attn * r1
        x1 = x_ref[...].astype(F32) + na * gpost_ref[...]
        r2 = lax.rsqrt(row_mean(x1 * x1) + epsilon)
        n1 = x1 * r2
        h2 = (n1 * gpre_ref[...]).astype(BF)
        gate = mm(h2, wg_s[...])
        up = mm(h2, wu_s[...])
        th = jnp.tanh(GELU_C * (gate + GELU_K * gate * gate * gate))
        half = 0.5 * (1.0 + th)
        gl = gate * half
        slope = half + 0.5 * gate * (1.0 - th * th) * (GELU_C * (1.0 + 3.0 * GELU_K * gate * gate))
        act = (gl * up).astype(BF)
        f = mm(act, wd_s[...])
        r3 = lax.rsqrt(row_mean(f * f) + epsilon)
        nf = f * r3
        res_ref[...] = (live * (x1 + nf * gffn_ref[...])).astype(BF)
        dy = live * ct_ref[...].astype(F32)
        gain_s[0] += fold_rows(dy * nf)
        df = norm_back(dy * gffn_ref[...], nf, r3).astype(BF)
        dact = mm_bt(df, wd_s[...])
        ad_s[...] += mm_at(act, df)
        dgate = (dact * up * slope).astype(BF)
        dup = (dact * gl).astype(BF)
        ag_s[...] += mm_at(h2, dgate)
        au_s[...] += mm_at(h2, dup)
        dh2 = mm_bt(dgate, wg_s[...]) + mm_bt(dup, wu_s[...])
        gain_s[1] += fold_rows(dh2 * n1)
        dx1 = dy + norm_back(dh2 * gpre_ref[...], n1, r2)
        dx1_ref[...] = dx1
        gain_s[2] += fold_rows(dx1 * na)
        dattn = norm_back(dx1 * gpost_ref[...], na, r1).astype(BF)
        ao_s[...] += mm_at(ob, dattn)
        dob_ref[...] = mm_bt(dattn, wo_s[...]).astype(BF)

    @pl.when(tile >= tiles)
    def _():
        pack.pack(tile - tiles, core_ref[0], [ag_s, au_s], [ao_s, ad_s], keep_ref, send_ref)
        dgains_ref[...] = gain_s[...]


def backward_kernel(
    pack, heads, tiles,
    lens_ref, starts_ref, core_ref, w_ref, x_ref, dx1_ref, h1_ref, qraw_ref, kraw_ref, qn_ref, dob_ref,
    k_ref, v_ref, cos_ref, sin_ref, gin_ref, gq_ref, gk_ref,
    gt_ref, dgin_ref, dgq_ref, dgk_ref, keep_ref, send_ref,
    dq_s, dk_s, dv_s, bias_s, acc_s, dqr_s,
):
    step = pl.program_id(0)
    hd = gk_ref.shape[1]
    wide = heads * hd

    @pl.when(step == 0)
    def _():
        for ref in (dk_s, dv_s, acc_s, dgin_ref, dgq_ref, dgk_ref):
            ref[...] = jnp.zeros(ref.shape, F32)

    for c in range(tiles):

        @pl.when(step == tiles - 1 - c)
        def _():
            span = (c + 1) * TILE
            slot = c * TILE + lax.broadcasted_iota(jnp.int32, (1, TILE), 1)
            first, _ = slot_starts(slot, lens_ref, starts_ref)
            other = lax.broadcasted_iota(jnp.int32, (span, TILE), 0)
            bias_s[:span, :] = jnp.where((other >= first) & (other <= slot), 0.0, BIG)
            for h in range(heads):
                q = qn_ref[:, h * hd : (h + 1) * hd]
                dob = dob_ref[:, h * hd : (h + 1) * hd]
                s = mm_bt(k_ref[:span, :], q) + bias_s[:span, :]
                e = jnp.exp(s - jnp.max(s, axis=0, keepdims=True))
                p = e * (1.0 / jnp.sum(e, axis=0, keepdims=True))
                dv_s[:span, :] += mm(p.astype(BF), dob)
                dp = mm_bt(v_ref[:span, :], dob)
                ds = (p * (dp - jnp.sum(p * dp, axis=0, keepdims=True))).astype(BF)
                dk_s[:span, :] += mm(ds, q)
                dq_s[:, h * hd : (h + 1) * hd] = mm_at(ds, k_ref[:span, :])

    @pl.when(step < tiles)
    def _():
        at = pl.multiple_of((tiles - 1 - step) * TILE, TILE)
        cos, sin = cos_ref[...], sin_ref[...]
        for h in range(heads):
            d = turn_back(dq_s[:, h * hd : (h + 1) * hd], cos, sin) * 0.0625
            part = qraw_ref[:, h * hd : (h + 1) * hd]
            scale = lax.rsqrt(row_mean(part * part) + epsilon)
            unit = part * scale
            dgq_ref[...] += fold_rows(d * unit)
            dqr_s[:, h * hd : (h + 1) * hd] = norm_back(d * gq_ref[...], unit, scale).astype(BF)
        d = turn_back(dk_s[pl.ds(at, TILE), :], cos, sin)
        part = kraw_ref[...]
        scale = lax.rsqrt(row_mean(part * part) + epsilon)
        unit = part * scale
        dgk_ref[...] += fold_rows(d * unit)
        dqr_s[:, wide : wide + hd] = norm_back(d * gk_ref[...], unit, scale).astype(BF)
        dqr_s[:, wide + hd :] = dv_s[pl.ds(at, TILE), :].astype(BF)
        acc_s[...] += mm_at(h1_ref[...], dqr_s[...])
        dh1 = mm_bt(dqr_s[...], w_ref[...])
        x = x_ref[...].astype(F32)
        scale = lax.rsqrt(row_mean(x * x) + epsilon)
        unit = x * scale
        dgin_ref[...] += fold_rows(dh1 * unit)
        gt_ref[...] = dx1_ref[...] + norm_back(dh1 * gin_ref[...], unit, scale)

    @pl.when(step >= tiles)
    def _():
        accs = [acc_s.at[:, :wide], acc_s.at[:, wide : wide + hd], acc_s.at[:, wide + hd :]]
        pack.pack(step - tiles, core_ref[0], accs, [], keep_ref, send_ref)


def smem():
    return pl.BlockSpec(memory_space=pltpu.SMEM)


def whole(shape):
    zeros = (0,) * len(shape)
    return pl.BlockSpec(shape, lambda s: zeros)


def resident(shape):
    zeros = (0,) * len(shape)
    return pl.BlockSpec(shape, lambda s: zeros, pipeline_mode=pl.Buffered(1))


def params(megabytes):
    return pltpu.CompilerParams(
        dimension_semantics=("arbitrary",), vmem_limit_bytes=megabytes * 1024 * 1024
    )


def shape(dims, kind):
    return jax.ShapeDtypeStruct(dims, kind)


def run_forward(pack, heads, lens, starts, gathered, tokens, cos, sin, gin, gq, gk):
    slots, model = tokens.shape
    hd = gk.shape[1]
    wide = heads * hd
    cols = wide + 2 * hd
    last = pack.steps - 1

    def tile_spec(width):
        return pl.BlockSpec((TILE, width), lambda s: (jnp.maximum(s - pack.steps, 0), 0))

    packed = pl.BlockSpec(
        (pack.chips_per_step, 2, gathered.shape[2], LANES), lambda s: (jnp.minimum(s, last), 0, 0, 0)
    )
    return pl.pallas_call(
        functools.partial(forward_kernel, pack, heads),
        grid=(pack.steps + slots // TILE,),
        in_specs=[
            smem(), smem(), packed, tile_spec(model), tile_spec(hd // 2), tile_spec(hd // 2),
            whole((1, model)), whole((1, hd)), whole((1, hd)),
        ],
        out_specs=[
            pl.BlockSpec((STEP_ROWS, cols), lambda s: (jnp.minimum(s, last), 0)),
            tile_spec(model), tile_spec(wide), tile_spec(hd), tile_spec(wide), tile_spec(hd), tile_spec(hd), tile_spec(wide),
        ],
        out_shape=[
            shape((model, cols), BF), shape((slots, model), BF), shape((slots, wide), F32),
            shape((slots, hd), F32), shape((slots, wide), BF), shape((slots, hd), BF), shape((slots, hd), BF),
            shape((slots, wide), BF),
        ],
        scratch_shapes=[
            pltpu.VMEM((model, cols), BF), pltpu.VMEM((slots, hd), BF), pltpu.VMEM((slots, hd), BF),
            pltpu.VMEM((TILE, slots), F32),
        ],
        compiler_params=params(48),
        cost_estimate=pl.CostEstimate(
            flops=2 * slots * model * cols + 4 * slots * slots * wide // 2,
            bytes_accessed=16 * 1024 * 1024, transcendentals=heads * slots * slots,
        ),
        name="attention_forward",
    )(lens, starts, gathered, tokens, cos, sin, gin, gq, gk)


def run_middle(pack, lens, starts, core, gathered, tokens, ob, cotangent, gpost, gpre, gffn):
    slots, model = tokens.shape
    wide = ob.shape[1]
    ff = pack.narrow[0][1]
    tiles = slots // TILE
    last = pack.steps - 1

    def tile_spec(width):
        return pl.BlockSpec((TILE, width), lambda s: (jnp.clip(s - pack.steps, 0, tiles - 1), 0))

    def out_packed():
        return pl.BlockSpec(
            (pack.chips_per_step, pack.used, LANES),
            lambda s: (jnp.maximum(s - pack.steps - tiles, 0), 0, 0),
        )

    packed = pl.BlockSpec(
        (pack.chips_per_step, 2, gathered.shape[2], LANES), lambda s: (jnp.minimum(s, last), 0, 0, 0)
    )
    return pl.pallas_call(
        functools.partial(middle_kernel, pack, tiles),
        grid=(2 * pack.steps + tiles,),
        in_specs=[
            smem(), smem(), smem(), packed, tile_spec(model), tile_spec(wide), tile_spec(model),
            whole((1, model)), whole((1, model)), whole((1, model)),
        ],
        out_specs=[
            tile_spec(model), tile_spec(model), tile_spec(wide), whole((3, 8, model)), out_packed(), out_packed(),
        ],
        out_shape=[
            shape((slots, model), BF), shape((slots, model), F32), shape((slots, wide), BF),
            shape((3, 8, model), F32),
            shape((pack.chips, pack.used, LANES), BF), shape((pack.chips, pack.used, LANES), BF),
        ],
        scratch_shapes=[
            pltpu.VMEM((model, ff), BF), pltpu.VMEM((model, ff), BF), pltpu.VMEM((wide, model), BF),
            pltpu.VMEM((ff, model), BF),
            pltpu.VMEM((model, ff), F32), pltpu.VMEM((model, ff), F32), pltpu.VMEM((wide, model), F32),
            pltpu.VMEM((ff, model), F32), pltpu.VMEM((3, 8, model), F32),
        ],
        compiler_params=params(60),
        cost_estimate=pl.CostEstimate(
            flops=6 * slots * model * (3 * ff + wide), bytes_accessed=36 * 1024 * 1024,
            transcendentals=slots * ff,
        ),
        name="output_and_ffn",
    )(lens, starts, core, gathered, tokens, ob, cotangent, gpost, gpre, gffn)


def run_backward(pack, heads, lens, starts, core, weights, tokens, dx1, h1, qraw, kraw, qn, dob, kn, v, cos, sin, gin, gq, gk):
    slots, model = tokens.shape
    hd = gk.shape[1]
    wide = heads * hd
    cols = wide + 2 * hd
    tiles = slots // TILE

    def tile_spec(width):
        return pl.BlockSpec((TILE, width), lambda s: (jnp.maximum(tiles - 1 - s, 0), 0))

    def out_packed():
        return pl.BlockSpec(
            (pack.chips_per_step, pack.used, LANES), lambda s: (jnp.maximum(s - tiles, 0), 0, 0)
        )

    return pl.pallas_call(
        functools.partial(backward_kernel, pack, heads, tiles),
        grid=(tiles + pack.steps,),
        in_specs=[
            smem(), smem(), smem(), resident((model, cols)), tile_spec(model), tile_spec(model), tile_spec(model),
            tile_spec(wide), tile_spec(hd), tile_spec(wide), tile_spec(wide), resident((slots, hd)), resident((slots, hd)),
            tile_spec(hd // 2), tile_spec(hd // 2), whole((1, model)), whole((1, hd)), whole((1, hd)),
        ],
        out_specs=[
            tile_spec(model), whole((8, model)), whole((8, hd)), whole((8, hd)), out_packed(), out_packed(),
        ],
        out_shape=[
            shape((slots, model), F32), shape((8, model), F32), shape((8, hd), F32), shape((8, hd), F32),
            shape((pack.chips, pack.used, LANES), BF), shape((pack.chips, pack.used, LANES), BF),
        ],
        scratch_shapes=[
            pltpu.VMEM((TILE, wide), F32), pltpu.VMEM((slots, hd), F32), pltpu.VMEM((slots, hd), F32),
            pltpu.VMEM((slots, TILE), F32), pltpu.VMEM((model, cols), F32), pltpu.VMEM((TILE, cols), BF),
        ],
        compiler_params=params(56),
        cost_estimate=pl.CostEstimate(
            flops=4 * slots * model * cols + 10 * slots * slots * wide // 2,
            bytes_accessed=24 * 1024 * 1024, transcendentals=heads * slots * slots,
        ),
        name="attention_backward",
    )(lens, starts, core, weights, tokens, dx1, h1, qraw, kraw, qn, dob, kn, v, cos, sin, gin, gq, gk)


class Mover:
    def __init__(self, device_count):
        self.n = device_count
        self.chips = device_count // 2
        self.digits = 0
        while 4 ** (self.digits + 1) <= self.chips:
            self.digits += 1
        me = lax.axis_index(AX)
        self.core = me % 2
        self.chip = me // 2

    def swap(self, value, mask=1):
        return lax.ppermute(value, AX, [(i, i ^ mask) for i in range(self.n)])

    def in_core_order(self, mine, other):
        first = self.core == 0
        return jnp.where(first, mine, other), jnp.where(first, other, mine)

    def trade_halves(self, narrow):
        halves = [jnp.split(w, 2, axis=1) for w in narrow]
        low = jnp.concatenate([h[0] for h in halves], axis=1)
        high = jnp.concatenate([h[1] for h in halves], axis=1)
        first = self.core == 0
        mine = jnp.where(first, low, high)
        other = self.swap(jnp.where(first, high, low))
        return jnp.concatenate(self.in_core_order(mine, other), axis=0)

    def gather(self, blocks):
        tiles = [b.reshape(b.shape[0], -1, LANES).transpose(1, 0, 2).reshape(-1, LANES) for b in blocks]
        whole_array = lax.all_gather(jnp.concatenate(tiles, axis=0), AX, axis=0)
        return whole_array.reshape(self.chips, 2, -1, LANES)

    def cores(self, keep, send):
        return keep.astype(F32) + self.swap(send).astype(F32)

    def digit(self, total, digit):
        low = total.astype(BF).reshape(total.shape[0] // 4, 4, -1, LANES)
        here = (self.chip >> (2 * digit)) % 4
        moved = [
            self.swap(
                lax.dynamic_index_in_dim(low, here ^ j, 1, keepdims=False), j << (2 * digit + 1)
            )
            for j in (1, 2, 3)
        ]
        total = lax.dynamic_index_in_dim(total.reshape(low.shape), here, 1, keepdims=False)
        for m in moved:
            total = total + m.astype(F32)
        return total

    def split_narrow(self, total, pack):
        rows = pack.pair // 2
        count = sum(cols // (2 * LANES) for _, cols in pack.narrow)
        tiles = total[: count * pack.pair].reshape(-1, 2, rows, LANES)
        mine = lax.dynamic_index_in_dim(tiles, self.core, 1, keepdims=False)
        other = self.swap(lax.dynamic_index_in_dim(tiles, 1 - self.core, 1, keepdims=False))
        halves = self.in_core_order(mine, other)
        outs, at = [], 0
        for _, cols in pack.narrow:
            t = cols // (2 * LANES)
            both = jnp.stack([h[at : at + t] for h in halves])
            outs.append(both.transpose(2, 0, 1, 3).reshape(rows, cols))
            at += t
        return outs

    def split_tall(self, total, pack):
        outs = []
        for (rows, cols), at in zip(pack.tall, pack.tall_at):
            own, t = rows // self.n, cols // LANES
            piece = total[at : at + t * own].reshape(t, own, LANES)
            outs.append(piece.transpose(1, 0, 2).reshape(own, cols))
        return outs


def on_device(
    device_count,
    tokens,
    cotangent,
    seq_lens,
    seq_starts,
    input_gain,
    w_query,
    w_key,
    w_value,
    query_gain,
    key_gain,
    w_output,
    attn_post_gain,
    ffn_pre_gain,
    w_gate,
    w_up,
    w_down,
    ffn_post_gain,
):
    mover = Mover(device_count)
    chips = mover.chips
    slots, model = tokens.shape
    hd = w_key.shape[1]
    heads = w_query.shape[1] // hd
    ffn = Pack(
        chips,
        [(model, w_gate.shape[1]), (model, w_up.shape[1])],
        [(w_output.shape[0] * device_count, model), (w_down.shape[0] * device_count, model)],
        0,
    )
    attn = Pack(chips, [(model, heads * hd), (model, hd), (model, hd)], [], ffn.used)

    gains = [input_gain, query_gain, key_gain, attn_post_gain, ffn_pre_gain, ffn_post_gain]
    flat = jnp.concatenate(gains)
    flat = jnp.pad(flat, (0, 8 * LANES - flat.shape[0])).reshape(8, LANES)
    narrow = mover.trade_halves([w_gate, w_up, w_query, w_key, w_value])
    split = w_gate.shape[1]
    gathered = mover.gather([narrow[:, :split], w_output, w_down, narrow[:, split:], flat])
    flat = gathered[:, :, ffn.used + attn.used :].reshape(device_count, 8 * LANES)
    vectors, at = [], 0
    for g in gains:
        vectors.append(flat[:, at : at + g.shape[0]].reshape(1, -1).astype(F32))
        at += g.shape[0]
    gin, gq, gk, gpost, gpre, gffn = vectors

    slot = jnp.arange(slots, dtype=jnp.int32)
    inside = (slot[None, :] >= seq_starts[:, None]) & (
        slot[None, :] < seq_starts[:, None] + seq_lens[:, None]
    )
    offset = jnp.sum(jnp.where(inside, seq_starts[:, None], 0), axis=0)
    frequency = rope_base ** (-2.0 * jnp.arange(hd // 2, dtype=F32) / hd)
    angles = (slot - offset).astype(F32)[:, None] * frequency[None, :]
    cos, sin = jnp.cos(angles), jnp.sin(angles)
    core = mover.core.astype(jnp.int32).reshape(1)

    weights, h1, qraw, kraw, qn, kn, v, ob = run_forward(
        attn, heads, seq_lens, seq_starts, gathered, tokens, cos, sin, gin, gq, gk
    )
    result, dx1, dob, dgains, keep, send = run_middle(
        ffn, seq_lens, seq_starts, core, gathered, tokens, ob, cotangent, gpost, gpre, gffn
    )
    ffn_sum = mover.cores(keep, send)
    dob, ffn_sum = lax.optimization_barrier((dob, ffn_sum))
    grad_tokens, dgin, dgq, dgk, keep, send = run_backward(
        attn, heads, seq_lens, seq_starts, core, weights, tokens, dx1, h1, qraw, kraw, qn, dob, kn, v,
        cos, sin, gin, gq, gk,
    )
    dffn, dpre, dpost = (jnp.sum(dgains[i], axis=0) for i in range(3))
    grads = [jnp.sum(dgin, axis=0), jnp.sum(dgq, axis=0), jnp.sum(dgk, axis=0), dpost, dpre, dffn]
    flat = jnp.concatenate([g.reshape(device_count, -1) for g in grads], axis=1).astype(BF)
    flat = jnp.pad(flat, ((0, 0), (0, 8 * LANES - flat.shape[1]))).reshape(chips, 2, 8, LANES)
    keep = jnp.concatenate(
        [keep, lax.dynamic_index_in_dim(flat, mover.core, 1, keepdims=False)], axis=1
    )
    send = jnp.concatenate(
        [send, lax.dynamic_index_in_dim(flat, 1 - mover.core, 1, keepdims=False)], axis=1
    )
    attn_sum = mover.cores(keep, send)
    for d in range(mover.digits):
        ffn_sum = mover.digit(ffn_sum, d)
        attn_sum = mover.digit(attn_sum, d)
    ffn_sum, attn_sum = ffn_sum[0], attn_sum[0]
    own_gate, own_up = mover.split_narrow(ffn_sum, ffn)
    own_output, own_down = mover.split_tall(ffn_sum, ffn)
    own_query, own_key, own_value = mover.split_narrow(attn_sum, attn)
    flat = attn_sum[attn.used :].reshape(-1)
    owned, at = [], 0
    for g in gains:
        owned.append(flat[at : at + g.shape[0]])
        at += g.shape[0]
    own_gin, own_gq, own_gk, own_gpost, own_gpre, own_gffn = owned
    return (
        result, grad_tokens, own_gin, own_query, own_key, own_value, own_gq, own_gk, own_output, own_gpost,
        own_gpre, own_gate, own_up, own_down, own_gffn,
    )


def solution(mesh):
    rows, flat = P(AX, None), P(AX)
    device_count = mesh.shape[AX]

    def block(*arrays):
        return on_device(device_count, *arrays)

    return jax.shard_map(
        block,
        mesh=mesh,
        in_specs=(
            rows, rows, flat, flat, flat, rows, rows, rows, flat, flat, rows, flat, flat, rows, rows, rows, flat,
        ),
        out_specs=(
            rows, rows, flat, rows, rows, rows, flat, flat, rows, flat, flat, rows, rows, rows, flat,
        ),
        check_vma=False,
    )
```

time: 502 us -> 380 us (0.76); the launches traced: 492 us -> 377 us
  Pallas kernels: 0 us -> 122 us
  matrix products: 118 us -> 0 us
  local copies, waits for them, and re-layouts: 112 us -> 32.6 us
  other arithmetic: 62.2 us -> 22.3 us
    pallas_call x0 -> x3, Pallas kernels: none -> 122 us  [the longest x1 60.2 us: run_middle(): pl.pallas_call(functools.partial(middle_kernel, pack, tiles), grid=(2 * p...]
    dot_general x28 -> x0, matrix products: 118 us -> none  [the longest x7 26.8 us: times_transposed(): lax.dot_general(left_side, right_side, (((1,), (1,)), ((), ())), preferre...]
    reshape x30 -> x15, local copies, waits for them, and re-layouts: 39.5 us -> 4.6 us  [the longest x3 1.93 us: gather(): b.reshape(b.shape[0], -1, LANES).transpose(1, 0, 2).reshape(-1, LANES)]
    convert_element_type x13 -> x6, other arithmetic: 29.4 us -> 6.28 us  [the longest x3 6.12 us: digit(): low = total.astype(BF).reshape(total.shape[0] // 4, 4, -1, LANES)]
    transpose x17 -> x7, local copies, waits for them, and re-layouts: 19.3 us -> 0.12 us  [the longest x4 0.08 us: gather(): b.reshape(b.shape[0], -1, LANES).transpose(1, 0, 2).reshape(-1, LANES)]
    unnamed x184 -> x56, local copies, waits for them, and re-layouts: 25.7 us -> 13.2 us
    reduce_sum x8 -> x5, other arithmetic: 14.4 us -> 3.06 us  [the longest x1 0.79 us: on_device(): dffn, dpre, dpost = (jnp.sum(dgains[i], axis=0) for i in range(3))]
    slice x10 -> x7, local copies, waits for them, and re-layouts: 10.1 us -> 2.07 us  [the longest x2 1.18 us: on_device(): owned.append(flat[at:at + g.shape[0]])]
  transfers between devices with their start and end apart: 20 -> 18, of which waited for: 11 -> 11; matrix products, arithmetic and copies ran while one was open for 23% -> 6% of each run, Pallas kernels for 0% -> 0%
where the time goes in v2:
time: 380 us; the launch traced here: 377 us
  waiting for transfers between devices  168 us (44%)
  Pallas kernels  122 us (32%)
  local copies, waits for them, and re-layouts  32.6 us (9%)
  other arithmetic  22.3 us (6%)
  starting transfers between devices  17.4 us (5%)
  between operations  14.8 us (4%)
    all_gather x1, waiting for transfers between devices, gather(): whole_array = lax.all_gather(jnp.concatenate(tiles, axis=0), AX, axis=0)  88.8 us
    ppermute x17, waiting for transfers between devices, swap(): return lax.ppermute(value, AX, [(i, i ^ mask) for i in range(self.n)])  79.5 us
    pallas_call x1, Pallas kernels, run_middle(): pl.pallas_call(functools.partial(middle_kernel, pack, tiles), grid=(2 * p...  60.2 us
    pallas_call x1, Pallas kernels, run_backward(): pl.pallas_call(functools.partial(backward_kernel, pack, heads, tiles), gr...  42.3 us
    pallas_call x1, Pallas kernels, run_forward(): pl.pallas_call(functools.partial(forward_kernel, pack, heads), grid=(pack...  19.1 us
    ppermute x17, starting transfers between devices, swap(): return lax.ppermute(value, AX, [(i, i ^ mask) for i in range(self.n)])  17.4 us
    unnamed x56, local copies, waits for them, and re-layouts  13.2 us
  transfers between devices with their start and end apart: 18, of which 11 were waited for; matrix products, arithmetic and copies ran while one was open for 6% of the time, Pallas kernels for 0%

profile of v2, /device:TPU:9, one launch (start us, length us, event | category | flops | bytes accessed | tf_op | source)
XLA Modules:
  0.0 376.9 jit_solution(5204902057835507152)
XLA Ops:
  7.2 0.8 slice_dynamic-update-slice_fusion.3
  8.1 0.8 slice_dynamic-update-slice_fusion.2
  8.9 0.8 constant_dynamic-update-slice_fusion.2
  9.7 0.7 constant_dynamic-update-slice_fusion.1
  10.4 0.7 constant_dynamic-update-slice_fusion
  11.1 0.7 collective-permute-start
  11.9 0.8 reshape.276
  12.7 1.0 reshape.278
  13.8 4.1 %concatenate.28 = bf16[96]{0:T(256)(128)(2,1)S(1)} concatenate(bf16[20]{0:T(256)(128)(2,1)} %param.21, bf16[8]{0:T(256)(128)(2,1)} %param.25, bf16[8]{0:T(256)(128)(2,1)} %param.26, bf16[20]{0:T(256)(128)(2,1)} %param.28, bf16[20]{0:T(256)(128)(2,1)} %param.29, bf16[20]{0:T(256)(128)(2,1)} %param.33), dimensions={0} | concatenate | bytes 384 | tf_op jit(solution)/shard_map/concatenate | solution.py:600
  18.3 0.7 copy-done.15
  19.2 1.9 multiply_sine_fusion
  21.1 88.8 %all-gather.3.cloned.1.call-done = bf16[43776,128]{1,0:T(8,128)(2,1)} async-done(((bf16[1368,128]{1,0:T(8,128)(2,1)}), bf16[43776,128]{1,0:T(8,128)(2,1)}) %all-gather.3.cloned.1.call-update) | async-done | bytes 11206672 | tf_op jit(solution)/shard_map/all_gather | solution.py:522
  109.9 0.8 slice.139
  111.2 0.7 reshape.310.gpost_ref
  111.9 0.7 reshape.311.gpre_ref
  112.6 0.7 reshape.312.gffn_ref
  113.3 19.1 %attention_forward.1 = (bf16[640,1536]{1,0:T(8,128)(2,1)}, bf16[1024,640]{1,0:T(8,128)(2,1)S(1)}, f32[1024,1024]{1,0:T(8,128)}, f32[1024,256]{1,0:T(8,128)S(1)},...) custom-call(s32[4]{0:T(128)S(1)} %copy-done.7, ...), custom_call_target="tpu_custom_call" | custom-call | flops 4160749568 | bytes 16777216 | tf_op jit(solution)/shard_map/attention_forward/pallas_call | solution.py:372
  132.4 1.1 copy-done.8
  133.5 1.0 copy-done.9
  134.4 0.8 copy-done.10
  135.2 0.8 copy-done.11
  136.1 60.2 %output_and_ffn.1 = (bf16[1024,640]{1,0:T(8,128)(2,1)}, f32[1024,640]{1,0:T(8,128)}, bf16[1024,1024]{1,0:T(8,128)(2,1)}, f32[3,8,640]{2,1,0:T(8,128)}, bf16[16,1...) custom-call(s32[4]{0:T(128)} %lens_ref.5, s32[4]{0:T(128)} %starts_ref.5, s32[1]{0:T(128)} %bitcast.core_ref, ...), custom_call_target="tpu_custom_call" | custom-call | flops 28185722880 | bytes 37748736 | tf_op jit(solution)/shard_map/output_and_ffn/pallas_call | solution.py:420
  196.5 0.8 slice_reduce_fusion
  197.7 6.7 %collective-permute-done.1 = bf16[16,1120,128]{2,1,0:T(8,128)(2,1)} collective-permute-done((bf16[16,1120,128]{2,1,0:T(8,128)(2,1)}, bf16[16,1120,128]{2,1,0:T(8,128)(2,1)}, u32[]{:S(2)}, u32[]{:S(2)}) %collective-permute-start.1) | collective-permute-done | bytes 4587552 | tf_op jit(solution)/shard_map/ppermute | solution.py:505
  204.3 4.9 %convert_add_fusion = f32[16,1120,128]{2,1,0:T(8,128)S(1)} fusion(bf16[16,1120,128]{2,1,0:T(8,128)(2,1)} %collective-permute-done.1, bf16[16,1120,128]{2,1,0:T(8,128)(2,1)} %get-tuple-element.46), kind=kLoop, calls=%fused_computation | loop fusion | flops 6881280 | bytes 18350080 | tf_op jit(solution)/shard_map/add | solution.py:526
  209.2 3.1 convert_element_type.127
  212.3 1.8 copy-done.12
  214.1 42.3 %attention_backward.1 = (f32[1024,640]{1,0:T(8,128)}, f32[8,640]{1,0:T(8,128)}, f32[8,256]{1,0:T(8,128)}, f32[8,256]{1,0:T(8,128)}, bf16[16,240,128]{2,1,0:T(8,128)(2,1)}, /*index=5*/bf16[16,240,128]{2,1,0:T(8,128)(2,1)}) custom-call(s32[4]{0:T(128)} %lens_ref.5, s32[4]{0:T(128)} %starts_ref.5, s32[1]{0:T(128)} %bitcast.core_ref, ...), custom_call_target="tpu_custom_call" | custom-call | flops 9395240960 | bytes 25165824 | tf_op jit(solution)/shard_map/attention_backward/pallas_call | solution.py:465
  256.4 0.7 reduce_sum.64
  257.2 0.7 reduce_sum.65
  258.1 0.7 reduce_sum.66
  259.0 2.3 pad_maximum_fusion
  261.6 3.7 dynamic-slice_bitcast_fusion.2
  265.3 1.2 collective-permute-start.10
  266.8 1.2 collective-permute-start.12
  268.0 1.8 convert_add_fusion.1
  269.8 1.2 collective-permute-start.3
  271.4 20.8 %collective-permute-done.10 = bf16[4,1120,128]{2,1,0:T(8,128)(2,1)S(1)} collective-permute-done((bf16[4,1120,128]{2,1,0:T(8,128)(2,1)}, bf16[4,1120,128]{2,1,0:T(8,128)(2,1)S(1)}, u32[]{:S(2)}, u32[]{:S(2)}) %collective-permute-start.10) | collective-permute-done | bytes 1146912 | tf_op jit(solution)/shard_map/ppermute | solution.py:505
  292.1 1.2 collective-permute-start.5
  293.3 24.4 %collective-permute-done.12 = bf16[4,1120,128]{2,1,0:T(8,128)(2,1)S(1)} collective-permute-done((bf16[4,1120,128]{2,1,0:T(8,128)(2,1)}, bf16[4,1120,128]{2,1,0:T(8,128)(2,1)S(1)}, u32[]{:S(2)}, u32[]{:S(2)}) %collective-permute-start.12) | collective-permute-done | bytes 1146912 | tf_op jit(solution)/shard_map/ppermute | solution.py:505
  317.7 1.0 copy-done.14
  318.7 2.9 fusion.8
  322.2 0.8 collective-permute-done.4
  323.0 5.6 %collective-permute-done.5 = bf16[4,248,128]{2,1,0:T(8,128)(2,1)S(1)} collective-permute-done((bf16[4,248,128]{2,1,0:T(8,128)(2,1)S(1)}, bf16[4,248,128]{2,1,0:T(8,128)(2,1)S(1)}, u32[]{:S(2)}, u32[]{:S(2)}) %collective-permute-start.5) | collective-permute-done | bytes 253984 | tf_op jit(solution)/shard_map/ppermute | solution.py:505
  329.4 1.5 collective-permute-start.7
  330.8 0.7 collective-permute-start.8
  331.5 0.8 constant_dynamic-slice_fusion.4
  332.3 1.4 collective-permute-start.13
  334.3 0.7 collective-permute-start.15
  335.0 1.1 collective-permute-done.8
  336.2 3.8 collective-permute-start.9
  341.8 0.6 maximum_bitcast_fusion.4
  342.4 3.2 collective-permute-done.13
  345.6 1.5 collective-permute-done.14
  347.2 14.6 %collective-permute-done.15 = bf16[1,1120,128]{2,1,0:T(8,128)(2,1)} collective-permute-done((bf16[1,1120,128]{2,1,0:T(8,128)(2,1)S(1)}, bf16[1,1120,128]{2,1,0:T(8,128)(2,1)}, u32[]{:S(2)}, u32[]{:S(2)}) %collective-permute-start.15) | collective-permute-done | bytes 286752 | tf_op jit(solution)/shard_map/ppermute | solution.py:505
  361.8 1.2 convert_add_fusion.2
  363.2 1.6 collective-permute-start.16
  364.9 0.6 copy.99
  365.5 0.6 copy.98
  366.2 0.7 reshape.295
  366.9 0.7 copy.112
  367.6 0.6 copy.114
  368.3 0.7 copy.101
  369.1 0.7 copy.100
  (112 shorter events, 7.2 us)
Async XLA Ops:
  7.2 102.7 %all-gather.3.cloned.1.call-start = ((), (), s32[]{:S(2)}) async-start(), calls=%async_computation | async-start | bytes 11556864 | tf_op jit(solution)/shard_map/all_gather | solution.py:522
  11.1 7.9 %copy-start.5 = (s32[4]{0:T(128)S(1)}, s32[4]{0:T(128)}, u32[]{:S(2)}) copy-start(s32[4]{0:T(128)} %starts_ref.5) | copy-start | bytes 52
  11.1 7.9 %copy-start.7 = (s32[4]{0:T(128)S(1)}, s32[4]{0:T(128)}, u32[]{:S(2)}) copy-start(s32[4]{0:T(128)} %lens_ref.5) | copy-start | bytes 52
  11.1 6.7 %collective-permute-start = (bf16[20,2816]{1,0:T(8,128)(2,1)S(1)}, bf16[20,2816]{1,0:T(8,128)(2,1)S(1)}, u32[]{:S(2)}, u32[]{:S(2)}) collective-permute-start(bf16[20,2816]{1,0:T(8,128)(2,1)S(1)} %broadcast_select_fusion.2), channel_id=1, source_target_pairs={{0,1},{1,0},{2,3},{3,2},{4,5},{5,4},{6,7},{7,6},{8,9},{9,8},{10,11... | collective-permute-start | bytes 337928 | tf_op jit(solution)/shard_map/ppermute | solution.py:505
  17.9 95.3 %copy-start.6 = (bf16[1024,640]{1,0:T(8,128)(2,1)S(1)}, bf16[1024,640]{1,0:T(8,128)(2,1)}, u32[]{:S(2)}) copy-start(bf16[1024,640]{1,0:T(8,128)(2,1)} %x_ref.5) | copy-start | bytes 3932164
  18.3 0.7 copy-start.15
  21.1 111.3 %copy-start = (f32[1024,128]{1,0:T(8,128)}, f32[1024,128]{1,0:T(8,128)S(1)}, u32[]{:S(2)}) copy-start(f32[1024,128]{1,0:T(8,128)S(1)} %get-tuple-element.114.sin_ref) | copy-start | bytes 1572868
  21.1 111.3 %copy-start.1 = (f32[1024,128]{1,0:T(8,128)}, f32[1024,128]{1,0:T(8,128)S(1)}, u32[]{:S(2)}) copy-start(f32[1024,128]{1,0:T(8,128)S(1)} %get-tuple-element.115.cos_ref) | copy-start | bytes 1572868
  111.0 21.4 %copy-start.2 = (f32[1,640]{1,0:T(1,128)}, f32[1,640]{1,0:T(1,128)S(1)}, u32[]{:S(2)}) copy-start(f32[1,640]{1,0:T(1,128)S(1)} %reshape.307.gin_ref) | copy-start | bytes 7684
  111.1 21.3 %copy-start.3 = (f32[1,256]{1,0:T(1,128)}, f32[1,256]{1,0:T(1,128)S(1)}, u32[]{:S(2)}) copy-start(f32[1,256]{1,0:T(1,128)S(1)} %reshape.308.gq_ref) | copy-start | bytes 3076
  111.2 21.2 %copy-start.4 = (f32[1,256]{1,0:T(1,128)}, f32[1,256]{1,0:T(1,128)S(1)}, u32[]{:S(2)}) copy-start(f32[1,256]{1,0:T(1,128)S(1)} %reshape.309.gk_ref) | copy-start | bytes 3076
  132.4 1.1 copy-start.8
  133.5 1.0 copy-start.9
  134.4 0.8 copy-start.10
  135.2 0.8 copy-start.11
  196.2 8.1 %collective-permute-start.1 = (bf16[16,1120,128]{2,1,0:T(8,128)(2,1)}, bf16[16,1120,128]{2,1,0:T(8,128)(2,1)}, u32[]{:S(2)}, u32[]{:S(2)}) collective-permute-start(bf16[16,1120,128]{2,1,0:T(8,128)(2,1)} %get-tuple-element.47), channel_id=1, source_target_pairs={{0,1},{1,0},{2,3},{3,2},{4,5},{5,4},{6,7},{7,6},{8,9},{9,8},{10,11... | collective-permute-start | bytes 13762568 | tf_op jit(solution)/shard_map/ppermute | solution.py:505
  209.2 4.9 %copy-start.12 = (f32[16,1120,128]{2,1,0:T(8,128)}, f32[16,1120,128]{2,1,0:T(8,128)S(1)}, u32[]{:S(2)}) copy-start(f32[16,1120,128]{2,1,0:T(8,128)S(1)} %convert_add_fusion) | copy-start | bytes 27525124
  261.3 6.6 %collective-permute-start.2 = (bf16[16,248,128]{2,1,0:T(8,128)(2,1)}, bf16[16,248,128]{2,1,0:T(8,128)(2,1)}, u32[]{:S(2)}, u32[]{:S(2)}) collective-permute-start(bf16[16,248,128]{2,1,0:T(8,128)(2,1)} %pad_maximum_fusion), channel_id=1, source_target_pairs={{0,1},{1,0},{2,3},{3,2},{4,5},{5,4},{6,7},{7,6},{8,9},{9,8},{10,11... | collective-permute-start | bytes 3047432 | tf_op jit(solution)/shard_map/ppermute | solution.py:505
  265.3 26.8 %collective-permute-start.10 = (bf16[4,1120,128]{2,1,0:T(8,128)(2,1)}, bf16[4,1120,128]{2,1,0:T(8,128)(2,1)S(1)}, u32[]{:S(2)}, u32[]{:S(2)}) collective-permute-start(bf16[4,1120,128]{2,1,0:T(8,128)(2,1)} %get-tuple-element.66), channel_id=1, source_target_pairs={{0,2},{1,3},{2,0},{3,1},{4,6},{5,7},{6,4},{7,5},{8,10},{9,11},{10,... | collective-permute-start | bytes 3440648 | tf_op jit(solution)/shard_map/ppermute | solution.py:505
  266.5 26.8 %collective-permute-start.11 = (bf16[4,1120,128]{2,1,0:T(8,128)(2,1)}, bf16[4,1120,128]{2,1,0:T(8,128)(2,1)S(1)}, u32[]{:S(2)}, u32[]{:S(2)}) collective-permute-start(bf16[4,1120,128]{2,1,0:T(8,128)(2,1)} %get-tuple-element.68), channel_id=1, source_target_pairs={{0,4},{1,5},{2,6},{3,7},{4,0},{5,1},{6,2},{7,3},{8,12},{9,13},{10,... | collective-permute-start | bytes 3440648 | tf_op jit(solution)/shard_map/ppermute | solution.py:505
  266.8 50.9 %collective-permute-start.12 = (bf16[4,1120,128]{2,1,0:T(8,128)(2,1)}, bf16[4,1120,128]{2,1,0:T(8,128)(2,1)S(1)}, u32[]{:S(2)}, u32[]{:S(2)}) collective-permute-start(bf16[4,1120,128]{2,1,0:T(8,128)(2,1)} %get-tuple-element.67), channel_id=1, source_target_pairs={{0,6},{1,7},{2,4},{3,5},{4,2},{5,3},{6,0},{7,1},{8,14},{9,15},{10,... | collective-permute-start | bytes 3440648 | tf_op jit(solution)/shard_map/ppermute | solution.py:505
  269.8 52.4 %collective-permute-start.3 = (bf16[4,248,128]{2,1,0:T(8,128)(2,1)S(1)}, bf16[4,248,128]{2,1,0:T(8,128)(2,1)S(1)}, u32[]{:S(2)}, u32[]{:S(2)}) collective-permute-start(bf16[4,248,128]{2,1,0:T(8,128)(2,1)S(1)} %get-tuple-element.74), channel_id=1, source_target_pairs={{0,2},{1,3},{2,0},{3,1},{4,6},{5,7},{6,4},{7,5},{8,10},{9,11},{10,... | collective-permute-start | bytes 761864 | tf_op jit(solution)/shard_map/ppermute | solution.py:505
  271.1 52.0 %collective-permute-start.4 = (bf16[4,248,128]{2,1,0:T(8,128)(2,1)S(1)}, bf16[4,248,128]{2,1,0:T(8,128)(2,1)S(1)}, u32[]{:S(2)}, u32[]{:S(2)}) collective-permute-start(bf16[4,248,128]{2,1,0:T(8,128)(2,1)S(1)} %get-tuple-element.76), channel_id=1, source_target_pairs={{0,4},{1,5},{2,6},{3,7},{4,0},{5,1},{6,2},{7,3},{8,12},{9,13},{10,... | collective-permute-start | bytes 761864 | tf_op jit(solution)/shard_map/ppermute | solution.py:505
  292.1 36.5 %collective-permute-start.5 = (bf16[4,248,128]{2,1,0:T(8,128)(2,1)S(1)}, bf16[4,248,128]{2,1,0:T(8,128)(2,1)S(1)}, u32[]{:S(2)}, u32[]{:S(2)}) collective-permute-start(bf16[4,248,128]{2,1,0:T(8,128)(2,1)S(1)} %get-tuple-element.75), channel_id=1, source_target_pairs={{0,6},{1,7},{2,4},{3,5},{4,2},{5,3},{6,0},{7,1},{8,14},{9,15},{10,... | collective-permute-start | bytes 761864 | tf_op jit(solution)/shard_map/ppermute | solution.py:505
  293.3 24.4 %copy-start.13 = (bf16[4,1120,128]{2,1,0:T(8,128)(2,1)}, bf16[4,1120,128]{2,1,0:T(8,128)(2,1)S(1)}, u32[]{:S(2)}) copy-start(bf16[4,1120,128]{2,1,0:T(8,128)(2,1)S(1)} %collective-permute-done.11) | copy-start | bytes 3440644
  317.7 1.0 copy-start.14
  328.8 5.4 %collective-permute-start.6 = (bf16[1,248,128]{2,1,0:T(8,128)(2,1)S(1)}, bf16[1,248,128]{2,1,0:T(8,128)(2,1)S(1)}, u32[]{:S(2)}, u32[]{:S(2)}) collective-permute-start(bf16[1,248,128]{2,1,0:T(8,128)(2,1)S(1)} %get-tuple-element.83), channel_id=1, source_target_pairs={{0,8},{1,9},{2,10},{3,11},{4,12},{5,13},{6,14},{7,15},{8,0},{9,1},... | collective-permute-start | bytes 190472 | tf_op jit(solution)/shard_map/ppermute | solution.py:505
  329.4 5.6 %collective-permute-start.7 = (bf16[1,248,128]{2,1,0:T(8,128)(2,1)S(1)}, bf16[1,248,128]{2,1,0:T(8,128)(2,1)S(1)}, u32[]{:S(2)}, u32[]{:S(2)}) collective-permute-start(bf16[1,248,128]{2,1,0:T(8,128)(2,1)S(1)} %get-tuple-element.85), channel_id=1, source_target_pairs={{0,16},{1,17},{2,18},{3,19},{4,20},{5,21},{6,22},{7,23},{8,24},{9,... | collective-permute-start | bytes 190472 | tf_op jit(solution)/shard_map/ppermute | solution.py:505
  330.8 5.3 %collective-permute-start.8 = (bf16[1,248,128]{2,1,0:T(8,128)(2,1)S(1)}, bf16[1,248,128]{2,1,0:T(8,128)(2,1)S(1)}, u32[]{:S(2)}, u32[]{:S(2)}) collective-permute-start(bf16[1,248,128]{2,1,0:T(8,128)(2,1)S(1)} %get-tuple-element.84), channel_id=1, source_target_pairs={{0,24},{1,25},{2,26},{3,27},{4,28},{5,29},{6,30},{7,31},{8,16},{9,... | collective-permute-start | bytes 190472 | tf_op jit(solution)/shard_map/ppermute | solution.py:505
  332.3 13.3 %collective-permute-start.13 = (bf16[1,1120,128]{2,1,0:T(8,128)(2,1)}, bf16[1,1120,128]{2,1,0:T(8,128)(2,1)}, u32[]{:S(2)}, u32[]{:S(2)}) collective-permute-start(bf16[1,1120,128]{2,1,0:T(8,128)(2,1)} %get-tuple-element.71), channel_id=1, source_target_pairs={{0,8},{1,9},{2,10},{3,11},{4,12},{5,13},{6,14},{7,15},{8,0},{9,1},... | collective-permute-start | bytes 860168 | tf_op jit(solution)/shard_map/ppermute | solution.py:505
  333.7 13.5 %collective-permute-start.14 = (bf16[1,1120,128]{2,1,0:T(8,128)(2,1)S(1)}, bf16[1,1120,128]{2,1,0:T(8,128)(2,1)}, u32[]{:S(2)}, u32[]{:S(2)}) collective-permute-start(bf16[1,1120,128]{2,1,0:T(8,128)(2,1)S(1)} %get-tuple-element.73), channel_id=1, source_target_pairs={{0,16},{1,17},{2,18},{3,19},{4,20},{5,21},{6,22},{7,23},{8,24},{9,... | collective-permute-start | bytes 860168 | tf_op jit(solution)/shard_map/ppermute | solution.py:505
  334.3 27.5 %collective-permute-start.15 = (bf16[1,1120,128]{2,1,0:T(8,128)(2,1)S(1)}, bf16[1,1120,128]{2,1,0:T(8,128)(2,1)}, u32[]{:S(2)}, u32[]{:S(2)}) collective-permute-start(bf16[1,1120,128]{2,1,0:T(8,128)(2,1)S(1)} %get-tuple-element.72), channel_id=1, source_target_pairs={{0,24},{1,25},{2,26},{3,27},{4,28},{5,29},{6,30},{7,31},{8,16},{9,... | collective-permute-start | bytes 860168 | tf_op jit(solution)/shard_map/ppermute | solution.py:505
  336.2 4.9 %collective-permute-start.9 = (f32[6,20,128]{2,1,0:T(8,128)S(1)}, f32[6,20,128]{2,1,0:T(8,128)S(1)}, u32[]{:S(2)}, u32[]{:S(2)}) collective-permute-start(f32[6,20,128]{2,1,0:T(8,128)S(1)} %dynamic-slice_bitcast_fusion.6), channel_id=1, source_target_pairs={{0,1},{1,0},{2,3},{3,2},{4,5},{5,4},{6,7},{7,6},{8,9},{9,8},{10,11... | collective-permute-start | bytes 184328 | tf_op jit(solution)/shard_map/ppermute | solution.py:505
  363.1 1.8 copy-start.17
  363.1 1.8 copy-start.16
  363.2 5.0 %collective-permute-start.16 = (f32[16,20,128]{2,0,1:T(8,128)S(1)}, f32[16,20,128]{2,0,1:T(8,128)S(1)}, u32[]{:S(2)}, u32[]{:S(2)}) collective-permute-start(f32[16,20,128]{2,0,1:T(8,128)S(1)} %bitcast.164), channel_id=1, source_target_pairs={{0,1},{1,0},{2,3},{3,2},{4,5},{5,4},{6,7},{7,6},{8,9},{9,8},{10,11... | collective-permute-start | bytes 491528 | tf_op jit(solution)/shard_map/ppermute | solution.py:505
Sparse Core Ops, SparseCore 0:
  19.2 90.6 all-gather.2
